TPU v7x, 128 devices: a whole 4x4x4 slice. The times are simulated.
128 devices in a mesh: face: 4 (over y), tile: 32 (over x, z, core).
Axes of the slice: x: 4, y: 4, z: 4, core: 2. Of those that a mesh axis runs over, the one named last changes fastest.
Arguments:
- latlon: bfloat16 [8192, 74, 128], P(('face', 'tile')), may hold values from -6 to 6
- intersection_weight: bfloat16 [8192, 4, 128, 128], P(('face', 'tile')), may hold values from -0.5 to 0.5
- target_dev: int32 [8192, 4], P(('face', 'tile')), may hold values from 0 to 127, all different within a row; in each aligned block of 64 rows (0 to 63, 64 to 127, ...) at most 2 rows name the same one
- target_piece: int32 [8192, 4], P(('face', 'tile')), may hold values from 0 to 63
- counts: int32 [8192], P(('face', 'tile')), may hold values from 1 to 4
- conv_weight: bfloat16 [9, 256, 74], replicated, may hold values from -0.25 to 0.25
- cotangent: bfloat16 [4, 256, 512, 512], P('face', None, 'tile'), may hold values from -6 to 6
Outputs:
- activation: bfloat16 [4, 256, 512, 512], P('face', None, 'tile')
- grad_conv: float32 [9, 256, 74], replicated
- grad_latlon: bfloat16 [8192, 74, 128], P(('face', 'tile'))
Inputs may be any that keep to these rules, and one draw needn't show every extreme that they name: `target_dev`: among the 4 entries of one block all owners differ; among the entries of one device's 64 blocks (aligned blocks of rows) no owner is named more than 2 times, a bound that some block reaches. Entries j >= counts[b] of block b are not live.
All inputs are finite; a program needn't handle non-finite values.
Results may differ from a plain program's by a relative error of at most 0.0091.
Values may be sent and summed in bfloat16 or wider, within the bound.
A program may use at most 192 MiB of HBM per device.

v0:
```python
import math

import jax
import jax.numpy as jnp
from jax import lax
from jax.sharding import PartitionSpec as P

C = 74
HID = 256
ROWS = 16
COLS = 512
PP = 128
K = 4
PIECES = 64


def padded_2(cells, sides, width):
    for axis, dim in sides:
        count = lax.axis_size(axis)
        head = lax.slice_in_dim(cells, 0, width, axis=dim)
        tail = lax.slice_in_dim(cells, cells.shape[dim] - width, cells.shape[dim], axis=dim)
        cells = jnp.concatenate(
            [
                lax.ppermute(tail, axis, [(i, (i + 1) % count) for i in range(count)]),
                cells,
                lax.ppermute(head, axis, [((i + 1) % count, i) for i in range(count)]),
            ],
            axis=dim,
        )
    return cells


def gelu_parts(value):
    inner = 0.7978845608 * (value + 0.044715 * value * value * value)
    tanh_part = jnp.tanh(inner)
    result = 0.5 * value * (1.0 + tanh_part)
    slope = 0.5 * (1.0 + tanh_part) + 0.5 * value * (1.0 - tanh_part * tanh_part) * 0.7978845608 * (
        1.0 + 0.134145 * value * value
    )
    return (result, slope)


def strip_edges(padded):
    tile_at = lax.axis_index("tile")
    last_tile = lax.axis_size("tile") - 1
    rows = jnp.arange(padded.shape[1], dtype=jnp.int32)
    outside = (rows == 0) & (tile_at == 0) | (rows == padded.shape[1] - 1) & (tile_at == last_tile)
    return jnp.where(outside[None, :, None], jnp.zeros((), padded.dtype), padded)


def to_owners(buffers):
    return (
        lax.all_to_all(buffers[0], ("face", "tile"), split_axis=0, concat_axis=0, tiled=True),
        lax.all_to_all(buffers[1], ("face", "tile"), split_axis=0, concat_axis=0, tiled=True),
    )


def to_sources(buffer):
    return lax.all_to_all(buffer, ("face", "tile"), split_axis=0, concat_axis=0, tiled=True)


def local(latlon, intersection_weight, target_dev, target_piece, counts, conv_weight, cotangent):
    faces = lax.axis_size("face")
    tiles = lax.axis_size("tile")
    devices = faces * tiles
    blocks = latlon.shape[0]
    slots = max(2, (blocks * K + devices - 1) // devices)
    live = jnp.arange(K, dtype=jnp.int32)[None, :] < counts[:, None]
    partial_value = jnp.einsum(
        "bcp,bjpq->bjcq", latlon, intersection_weight, preferred_element_type=jnp.float32
    )
    partial_value = jnp.where(live[:, :, None, None], partial_value, 0.0).astype(jnp.bfloat16)
    flat_dev = target_dev.reshape(-1)
    owner_hits = (flat_dev[:, None] == jnp.arange(devices, dtype=jnp.int32)[None, :]).astype(
        jnp.int32
    )
    earlier = jnp.cumsum(owner_hits, axis=0) - owner_hits
    slot = jnp.sum(earlier * owner_hits, axis=1)
    send = (
        jnp.zeros((devices, slots, C, PP), jnp.bfloat16)
        .at[flat_dev, slot]
        .set(partial_value.reshape(-1, C, PP))
    )
    send_piece = (
        jnp.full((devices, slots), -1, jnp.int32).at[flat_dev, slot].set(target_piece.reshape(-1))
    )
    recv, recv_piece = to_owners((send, send_piece))
    select = (
        recv_piece.reshape(-1)[None, :] == jnp.arange(PIECES, dtype=jnp.int32)[:, None]
    ).astype(jnp.bfloat16)
    field_sum = jnp.einsum(
        "pr,rcq->cpq", select, recv.reshape(-1, C, PP), preferred_element_type=jnp.float32
    )
    field = field_sum.astype(jnp.bfloat16).reshape(C, ROWS, COLS)
    field_pad = padded_2(field, (("tile", 1), ("face", 2)), 1)
    field_pad = strip_edges(field_pad)
    pre = jnp.zeros((HID, ROWS, COLS), jnp.float32)
    for k in range(9):
        ky, kx = divmod(k, 3)
        pre = pre + jnp.einsum(
            "oc,crw->orw",
            conv_weight[k],
            field_pad[:, ky : ky + ROWS, kx : kx + COLS],
            preferred_element_type=jnp.float32,
        )
    result, slope = gelu_parts(pre)
    activation = result.astype(jnp.bfloat16)[None]
    dpre = (cotangent[0].astype(jnp.float32) * slope).astype(jnp.bfloat16)
    terms = []
    for k in range(9):
        ky, kx = divmod(k, 3)
        terms.append(
            jnp.einsum(
                "orw,crw->oc",
                dpre,
                field_pad[:, ky : ky + ROWS, kx : kx + COLS],
                preferred_element_type=jnp.float32,
            )
        )
    grad_sum = lax.psum(jnp.stack(terms), ("face", "tile"))
    grad_conv = grad_sum * (1.0 / math.sqrt(devices * ROWS * COLS))
    dpre_pad = padded_2(dpre, (("tile", 1), ("face", 2)), 1)
    dpre_pad = strip_edges(dpre_pad)
    dfield_sum = jnp.zeros((C, ROWS, COLS), jnp.float32)
    for k in range(9):
        ky, kx = divmod(k, 3)
        dfield_sum = dfield_sum + jnp.einsum(
            "oc,orw->crw",
            conv_weight[k],
            dpre_pad[:, 2 - ky : 2 - ky + ROWS, 2 - kx : 2 - kx + COLS],
            preferred_element_type=jnp.float32,
        )
    dfield = dfield_sum.astype(jnp.bfloat16).reshape(C, PIECES, PP)
    reply = jnp.einsum("pr,cpq->rcq", select, dfield, preferred_element_type=jnp.float32).astype(
        jnp.bfloat16
    )
    back = to_sources(reply.reshape(devices, slots, C, PP))
    got = back[flat_dev, slot].reshape(blocks, K, C, PP)
    got = jnp.where(live[:, :, None, None], got, jnp.zeros((), jnp.bfloat16))
    grad_latlon = jnp.einsum(
        "bjcq,bjpq->bcp", got, intersection_weight, preferred_element_type=jnp.float32
    ).astype(jnp.bfloat16)
    return (activation, grad_conv, grad_latlon)


def solution(mesh):
    placed = (
        P(("face", "tile"), None, None),
        P(("face", "tile"), None, None, None),
        P(("face", "tile"), None),
        P(("face", "tile"), None),
        P(("face", "tile")),
        P(),
        P("face", None, "tile", None),
    )
    return jax.shard_map(
        local,
        mesh=mesh,
        in_specs=placed,
        out_specs=(P("face", None, "tile", None), P(), P(("face", "tile"), None, None)),
        check_vma=False,
    )
```

profile of v0, /device:TPU:1, one launch (start us, length us, event | category | flops | bytes accessed | tf_op | source)
XLA Modules:
  0.0 551.0 jit_solution(5217711497641472057)
XLA Ops:
  9.9 11.1 %scatter_fusion.1 = s32[128,2]{0,1:T(2,128)S(1)} fusion(s32[128,2]{0,1:T(2,128)S(1)} %broadcast_in_dim.76, s32[256]{0:T(256)S(1)} %bitcast.174, s32[256]{0:T(256)S(1)} %reshape.148), kind=kCustom, calls=%fused_computation.2 | custom fusion | bytes 5120 | tf_op jit(solution)/shard_map/scatter | solution.py:85
  21.7 11.5 %all-to-all-start.1 = ((s32[128,1,2]{2,1,0:T(1,128)}), s32[128,1,2]{2,1,0:T(1,128)S(1)}, u32[]{:S(2)}, u32[]{:S(2)}) async-start(s32[128,1,2]{2,1,0:T(1,128)} %copy.80), calls=%async_computation.1 | async-start | bytes 131072 | tf_op jit(solution)/shard_map/all_to_all | solution.py:54
  33.9 7.9 %select_convert_fusion = bf16[64,4,128,74]{2,3,1,0:T(8,128)(2,1)} fusion(pred[64,4]{1,0:T(8,128)(4,1)S(1)} %iota_compare_fusion.2, bf16[64,4,128,128]{3,2,1,0:T(8,128)(2,1)} %param.8, bf16[64,74,128,1]{2,0,1,3:T(8,128)(2,1)S(1)} %bitcast.172), kind=kOutput, calls=%fused_computation.5 | convolution fusion | flops 625606656 | bytes 14450944 | tf_op jit(solution)/shard_map/bcp,bjpq->bjcq/dot_general | solution.py:69
  44.8 37.2 %scatter_fusion = bf16[128,2,74,128]{3,2,1,0:T(8,128)(2,1)} fusion(bf16[128,2,74,128]{3,2,1,0:T(8,128)(2,1)} %broadcast_in_dim.73, s32[256]{0:T(256)S(1)} %bitcast.175, bf16[256,74,128]{2,1,0:T(8,128)(2,1)} %bitcast.179), kind=kCustom, calls=%fused_computation.1 | custom fusion | bytes 14551040 | tf_op jit(solution)/shard_map/scatter | solution.py:82
  82.0 8.5 %copy.77 = bf16[128,2,74,128]{3,1,2,0:T(2,128)(2,1)} copy(bf16[128,2,74,128]{3,2,1,0:T(8,128)(2,1)} %scatter_fusion) | data formatting | bytes 9699328 | tf_op jit(solution)/shard_map/scatter | solution.py:82
  90.5 10.6 %all-to-all-start = ((bf16[128,2,74,128]{3,1,2,0:T(2,128)(2,1)}), bf16[128,2,74,128]{3,1,2,0:T(2,128)(2,1)}, u32[]{:S(2)}, u32[]{:S(2)}) async-start(bf16[128,2,74,128]{3,1,2,0:T(2,128)(2,1)} %copy.77), calls=%async_computation | async-start | bytes 9699328 | tf_op jit(solution)/shard_map/all_to_all | solution.py:53
  102.6 58.0 %all-to-all-done = bf16[128,2,74,128]{3,1,2,0:T(2,128)(2,1)} async-done(((bf16[128,2,74,128]{3,1,2,0:T(2,128)(2,1)}), bf16[128,2,74,128]{3,1,2,0:T(2,128)(2,1)}, u32[]{:S(2)}, u32[]{:S(2)}) %all-to-all-start) | async-done | bytes 4849696 | tf_op jit(solution)/shard_map/all_to_all | solution.py:53
  160.6 10.0 %copy.78 = bf16[128,2,74,128]{3,1,0,2:T(2,128)(2,1)} copy(bf16[128,2,74,128]{3,1,2,0:T(2,128)(2,1)} %all-to-all-done) | data formatting | bytes 9699328 | tf_op jit(solution)/shard_map/all_to_all | solution.py:53
  184.3 8.0 %copy.84 = bf16[1,256,16,512]{1,3,2,0:T(8,128)(2,1)} copy(bf16[1,256,16,512]{3,2,1,0:T(8,128)(2,1)} %param.13) | data formatting | bytes 8388608 | tf_op args[6]
  195.0 5.7 %fusion.40 = f32[16,512,256]{2,1,0:T(8,128)} fusion(bf16[74,18,514]{2,0,1:T(8,128)(2,1)S(1)} %maximum_select_fusion.1, bf16[9,256,74]{1,2,0:T(8,128)(2,1)S(1)} %copy-done.7), kind=kOutput, calls=%fused_computation.53 | convolution fusion | flops 310378496 | bytes 9740288 | tf_op jit(solution)/shard_map/oc,crw->orw/dot_general | solution.py:100
  205.3 5.7 %fusion.48 = f32[16,512,256]{2,1,0:T(8,128)} fusion(bf16[74,18,514]{2,0,1:T(8,128)(2,1)S(1)} %maximum_select_fusion.1, bf16[9,256,74]{1,2,0:T(8,128)(2,1)S(1)} %copy-done.7), kind=kOutput, calls=%fused_computation.61 | convolution fusion | flops 310378496 | bytes 9740288 | tf_op jit(solution)/shard_map/oc,crw->orw/dot_general | solution.py:100
  211.0 5.7 %fusion.52 = f32[16,512,256]{2,1,0:T(8,128)} fusion(bf16[74,18,514]{2,0,1:T(8,128)(2,1)S(1)} %maximum_select_fusion.1, bf16[9,256,74]{1,2,0:T(8,128)(2,1)S(1)} %copy-done.7), kind=kOutput, calls=%fused_computation.65 | convolution fusion | flops 310378496 | bytes 9740288 | tf_op jit(solution)/shard_map/oc,crw->orw/dot_general | solution.py:100
  221.3 5.7 %fusion.60 = f32[16,512,256]{2,1,0:T(8,128)} fusion(bf16[74,18,514]{2,0,1:T(8,128)(2,1)S(1)} %maximum_select_fusion.1, bf16[9,256,74]{1,2,0:T(8,128)(2,1)S(1)} %copy-done.7), kind=kOutput, calls=%fused_computation.73 | convolution fusion | flops 310378496 | bytes 9740288 | tf_op jit(solution)/shard_map/oc,crw->orw/dot_general | solution.py:100
  227.0 5.7 %fusion.64 = f32[16,512,256]{2,1,0:T(8,128)} fusion(bf16[74,18,514]{2,0,1:T(8,128)(2,1)S(1)} %maximum_select_fusion.1, bf16[9,256,74]{1,2,0:T(8,128)(2,1)S(1)} %copy-done.7), kind=kOutput, calls=%fused_computation.77 | convolution fusion | flops 310378496 | bytes 9740288 | tf_op jit(solution)/shard_map/oc,crw->orw/dot_general | solution.py:100
  232.7 4.7 fusion.68
  237.5 24.8 %fusion.6 = (bf16[256,16,512]{0,2,1:T(8,128)(2,1)S(1)}, bf16[1,256,16,512]{1,3,2,0:T(8,128)(2,1)}) fusion(bf16[1,256,16,512]{1,3,2,0:T(8,128)(2,1)S(1)} %copy-done.4, bf16[9,256,74]{1,2,0:T(8,128)(2,1)S(1)} %copy-done.7, bf16[74,18,514]{2,0,1:T(8,128)(2,1)S(1)} %maximum_select_fusion.1, f32[16,512,256]{2,1,0:T(8,128)} %fusion.40, ...), kind=kOutput, calls=%fused_computation.12 | convolution fusion | flops 373293056 | bytes 81043456 | tf_op jit(solution)/shard_map/oc,crw->orw/dot_general | solution.py:100
  294.8 5.1 fusion.33
  308.0 7.9 %copy.104 = bf16[128,2,74,128]{3,1,2,0:T(2,128)(2,1)} copy(bf16[128,2,74,128]{3,1,0,2:T(2,128)(2,1)} %bitcast.176) | data formatting | bytes 9699328 | tf_op jit(solution)/shard_map/reshape | solution.py:137
  315.8 14.9 %all-to-all-start.2 = ((bf16[128,2,74,128]{3,1,2,0:T(2,128)(2,1)}), bf16[128,2,74,128]{3,1,2,0:T(2,128)(2,1)}, u32[]{:S(2)}, u32[]{:S(2)}) async-start(bf16[128,2,74,128]{3,1,2,0:T(2,128)(2,1)} %copy.104), calls=%async_computation.2 | async-start | bytes 9699328 | tf_op jit(solution)/shard_map/all_to_all | solution.py:59
  341.9 8.1 %copy.106 = bf16[1,256,16,512]{3,2,1,0:T(8,128)(2,1)} copy(bf16[1,256,16,512]{1,3,2,0:T(8,128)(2,1)} %get-tuple-element.15) | data formatting | bytes 8388608
  350.0 170.4 %all-reduce.2.cloned.1.call-done = f32[9,256,74]{1,2,0:T(8,128)} async-done(((f32[9,256,74]{1,2,0:T(8,128)}), f32[9,256,74]{1,2,0:T(8,128)}) %all-reduce.2.cloned.1.call-update) | async-done | bytes 682000 | tf_op jit(solution)/shard_map/psum | solution.py:120
  522.4 5.6 %copy.105 = bf16[128,2,74,128]{3,2,1,0:T(8,128)(2,1)} copy(bf16[128,2,74,128]{3,1,2,0:T(2,128)(2,1)} %all-to-all-done.2) | data formatting | bytes 9699328 | tf_op jit(solution)/shard_map/all_to_all | solution.py:59
  528.0 6.3 %gather_fusion = bf16[256,74,128]{2,1,0:T(8,128)(2,1)} fusion(bf16[128,2,74,128]{3,2,1,0:T(8,128)(2,1)} %copy.105, s32[256]{0:T(256)S(1)} %bitcast.178), kind=kCustom, calls=%fused_computation | custom fusion | bytes 9701376 | tf_op jit(solution)/shard_map/gather | solution.py:138
  534.3 8.0 %bitcast_convert_fusion = bf16[64,74,128]{2,1,0:T(8,128)(2,1)S(1)} fusion(bf16[64,4,128,128]{3,2,1,0:T(8,128)(2,1)} %param.8, bf16[64,4,74,128]{3,2,1,0:T(8,128)(2,1)} %bitcast.180, pred[64,4]{1,0:T(8,128)(4,1)S(1)} %iota_compare_fusion.2), kind=kOutput, calls=%fused_computation.40 | convolution fusion | flops 623788032 | bytes 14450944 | tf_op jit(solution)/shard_map/bjcq,bjpq->bcp/dot_general | solution.py:140
  (97 shorter events, 89.1 us)
Async XLA Ops:
  7.2 26.8 %copy-start = (bf16[64,74,128]{2,0,1:T(8,128)(2,1)S(1)}, bf16[64,74,128]{2,0,1:T(8,128)(2,1)}, u32[]{:S(2)}) copy-start(bf16[64,74,128]{2,0,1:T(8,128)(2,1)} %param.7) | copy-start | bytes 3637252
  21.7 68.8 %all-to-all-start.1 = ((s32[128,1,2]{2,1,0:T(1,128)}), s32[128,1,2]{2,1,0:T(1,128)S(1)}, u32[]{:S(2)}, u32[]{:S(2)}) async-start(s32[128,1,2]{2,1,0:T(1,128)} %copy.80), calls=%async_computation.1 | async-start | bytes 131072 | tf_op jit(solution)/shard_map/all_to_all | solution.py:54
  90.5 70.0 %all-to-all-start = ((bf16[128,2,74,128]{3,1,2,0:T(2,128)(2,1)}), bf16[128,2,74,128]{3,1,2,0:T(2,128)(2,1)}, u32[]{:S(2)}, u32[]{:S(2)}) async-start(bf16[128,2,74,128]{3,1,2,0:T(2,128)(2,1)} %copy.77), calls=%async_computation | async-start | bytes 9699328 | tf_op jit(solution)/shard_map/all_to_all | solution.py:53
  174.9 2.9 collective-permute-start
  176.3 3.9 collective-permute-start.1
  180.3 1.1 copy-start.5
  181.6 10.7 %collective-permute-start.2 = (bf16[74,18,1]{2,0,1:T(8,128)(2,1)S(1)}, bf16[74,18,1]{2,0,1:T(8,128)(2,1)S(1)}, u32[]{:S(2)}, u32[]{:S(2)}) collective-permute-start(bf16[74,18,1]{2,0,1:T(8,128)(2,1)S(1)} %get-tuple-element.20), channel_id=1, source_target_pairs={{0,32},{32,64},{64,96},{96,0},{1,33},{33,65},{65,97},{97,1},{2,34}... | collective-permute-start | bytes 8000 | tf_op jit(solution)/shard_map/ppermute | solution.py:24
  181.7 10.7 %collective-permute-start.3 = (bf16[74,18,1]{2,0,1:T(8,128)(2,1)S(1)}, bf16[74,18,1]{2,0,1:T(8,128)(2,1)S(1)}, u32[]{:S(2)}, u32[]{:S(2)}) collective-permute-start(bf16[74,18,1]{2,0,1:T(8,128)(2,1)S(1)} %get-tuple-element.21), channel_id=1, source_target_pairs={{32,0},{64,32},{96,64},{0,96},{33,1},{65,33},{97,65},{1,97},{34,2}... | collective-permute-start | bytes 8000 | tf_op jit(solution)/shard_map/ppermute | solution.py:26
  184.3 10.7 %copy-start.7 = (bf16[9,256,74]{1,2,0:T(8,128)(2,1)S(1)}, bf16[9,256,74]{1,2,0:T(8,128)(2,1)}, u32[]{:S(2)}) copy-start(bf16[9,256,74]{1,2,0:T(8,128)(2,1)} %param.12) | copy-start | bytes 1022980
  232.7 4.7 copy-start.4
  262.3 15.3 %copy-start.2 = (bf16[256,16,512]{0,2,1:T(8,128)(2,1)}, bf16[256,16,512]{0,2,1:T(8,128)(2,1)S(1)}, u32[]{:S(2)}) copy-start(bf16[256,16,512]{0,2,1:T(8,128)(2,1)S(1)} %get-tuple-element.14) | copy-start | bytes 12582916
  262.3 5.4 collective-permute-start.4
  263.6 5.8 %collective-permute-start.5 = (bf16[256,1,512]{0,2,1:T(8,128)(2,1)S(1)}, bf16[256,1,512]{0,2,1:T(8,128)(2,1)S(1)}, u32[]{:S(2)}, u32[]{:S(2)}) collective-permute-start(bf16[256,1,512]{0,2,1:T(8,128)(2,1)S(1)} %get-tuple-element.19), channel_id=1, source_target_pairs={{1,0},{2,1},{3,2},{4,3},{5,4},{6,5},{7,6},{8,7},{9,8},{10,9},{11,1... | collective-permute-start | bytes 786440 | tf_op jit(solution)/shard_map/ppermute | solution.py:26
  269.4 4.2 collective-permute-start.6
  269.5 4.1 collective-permute-start.7
  315.8 206.6 %all-to-all-start.2 = ((bf16[128,2,74,128]{3,1,2,0:T(2,128)(2,1)}), bf16[128,2,74,128]{3,1,2,0:T(2,128)(2,1)}, u32[]{:S(2)}, u32[]{:S(2)}) async-start(bf16[128,2,74,128]{3,1,2,0:T(2,128)(2,1)} %copy.104), calls=%async_computation.2 | async-start | bytes 9699328 | tf_op jit(solution)/shard_map/all_to_all | solution.py:59
  330.7 189.7 %all-reduce.2.cloned.1.call-start = ((), (), s32[]{:S(2)}) async-start(), calls=%async_computation.3 | async-start | bytes 1474560 | tf_op jit(solution)/shard_map/psum | solution.py:120
  330.7 3.5 copy-start.3
  341.0 0.9 copy-start.6
  534.3 9.4 %copy-start.1 = (bf16[64,74,128]{2,0,1:T(8,128)(2,1)S(1)}, bf16[64,74,128]{2,0,1:T(8,128)(2,1)}, u32[]{:S(2)}) copy-start(bf16[64,74,128]{2,0,1:T(8,128)(2,1)} %param.7) | copy-start | bytes 3637252
Sparse Core Ops, SparseCore 0:
  342.0 178.3 all-reduce.1
where the time goes:
time: 560 us; the launch traced here: 551 us
  waiting for transfers between devices  236 us (42%)
  matrix products  122 us (22%)
  local copies, waits for them, and re-layouts  119 us (21%)
  starting transfers between devices  48.3 us (9%)
  between operations  14.8 us (3%)
  other arithmetic  10.7 us (2%)
    psum x1, waiting for transfers between devices, local(): grad_sum = lax.psum(jnp.stack(terms), ('face', 'tile'))  170 us
    dot_general x9, matrix products, local(): jnp.einsum('oc,crw->orw', conv_weight[k], field_pad[:, ky:ky + ROWS, kx:k...  67.2 us
    all_to_all x1, waiting for transfers between devices, to_owners(): lax.all_to_all(buffers[0], ('face', 'tile'), split_axis=0, concat_axis=0,...  58 us
    scatter x2, local copies, waits for them, and re-layouts, local(): send = jnp.zeros((devices, slots, C, PP), jnp.bfloat16).at[flat_dev, slot...  45.7 us
    dot_general x9, matrix products, local(): jnp.einsum('oc,orw->crw', conv_weight[k], dpre_pad[:, 2 - ky:2 - ky + ROW...  22.4 us
    unnamed x26, local copies, waits for them, and re-layouts  22.1 us
    all_to_all x1, starting transfers between devices, to_sources(): lax.all_to_all(buffer, ('face', 'tile'), split_axis=0, concat_axis=0, til...  14.9 us
    all_to_all x1, starting transfers between devices, to_owners(): lax.all_to_all(buffers[1], ('face', 'tile'), split_axis=0, concat_axis=0,...  11.5 us
  transfers between devices with their start and end apart: 12, of which 7 were waited for; matrix products, arithmetic and copies ran while one was open for 16% of the time, Pallas kernels for 0%

commit v1 on v0

v1 whole, which is shorter than its diff:
```python
import functools
import math

import jax
import jax.numpy as jnp
from jax import lax
from jax.experimental import pallas as pl
from jax.experimental.pallas import tpu as pltpu
from jax.sharding import PartitionSpec as P

C = 74
CP = 80
SL = 76
HID = 256
ROWS = 16
COLS = 512
WIDE = 640
PP = 128
K = 4
PIECES = 64
DEVS = 128
GRP = 8
VMEM_LIMIT = 63 * 1024 * 1024
MESH = pl.DeviceIdType.MESH
f32 = jnp.float32
bf16 = jnp.bfloat16


def params(**kw):
    return pltpu.CompilerParams(vmem_limit_bytes=VMEM_LIMIT, **kw)


def whole(shape):
    zeros = (0,) * len(shape)
    return pl.BlockSpec(shape, lambda *a: zeros)


def partial_kernel(key_ref, lat_ref, w_ref, out_ref):
    step = pl.program_id(0)
    for g in range(GRP):
        parts = []
        for s in range(2):
            key = key_ref[(step * GRP + g) * 2 + s]
            entry = key >> 7
            alive = (key & 1).astype(f32)
            piece = ((key >> 1) & 63).astype(f32)
            value = jnp.dot(lat_ref[entry >> 2], w_ref[entry], preferred_element_type=f32)
            parts += [value * alive, jnp.full((SL - C, PP), piece, f32)]
        out_ref[g] = jnp.concatenate(parts, axis=0).astype(bf16)


def partial_products(keys, lat, weight):
    return pl.pallas_call(
        partial_kernel,
        grid_spec=pltpu.PrefetchScalarGridSpec(
            num_scalar_prefetch=1,
            grid=(DEVS // GRP,),
            in_specs=[whole(lat.shape), whole(weight.shape)],
            out_specs=pl.BlockSpec((GRP, 2 * SL, PP), lambda i, *a: (i, 0, 0)),
        ),
        out_shape=jax.ShapeDtypeStruct((DEVS, 2 * SL, PP), bf16),
        compiler_params=params(),
        name="partial",
    )(keys, lat, weight)


def gather_kernel(piece_ref, recv_ref, field_ref, pack_ref, acc_ref):
    step = pl.program_id(0)

    @pl.when(step == 0)
    def _():
        acc_ref[...] = jnp.zeros_like(acc_ref)

    for g in range(GRP):
        block = recv_ref[g].astype(f32)
        for s in range(2):
            piece = piece_ref[(step * GRP + g) * 2 + s]
            acc_ref[piece, :SL] += block[s * SL : (s + 1) * SL]

    @pl.when(step == pl.num_programs(0) - 1)
    def _():
        real = lax.broadcasted_iota(jnp.int32, (CP, PP), 0) < C
        lane = lax.broadcasted_iota(jnp.int32, (CP, PP), 1)
        left = jnp.zeros((CP, PP), f32)
        right = jnp.zeros((CP, PP), f32)
        for r in range(ROWS):
            for i in range(4):
                tile = jnp.where(real, acc_ref[r * 4 + i], 0.0)
                field_ref[r * 4 + i] = tile.astype(bf16)
                mine = (lane >> 1) == r
                if i == 0:
                    left = jnp.where(mine, pltpu.roll(tile, 2 * r, 1) if r else tile, left)
                if i == 3:
                    right = jnp.where(mine, pltpu.roll(tile, 2 * r + 2, 1), right)
        pack_ref[0] = left.astype(bf16)
        pack_ref[1] = right.astype(bf16)


def gather_field(pieces, recv):
    return pl.pallas_call(
        gather_kernel,
        grid_spec=pltpu.PrefetchScalarGridSpec(
            num_scalar_prefetch=1,
            grid=(DEVS // GRP,),
            in_specs=[pl.BlockSpec((GRP, 2 * SL, PP), lambda i, *a: (i, 0, 0))],
            out_specs=[whole((PIECES, CP, PP)), whole((2, CP, PP))],
            scratch_shapes=[pltpu.VMEM((PIECES, CP, PP), f32)],
        ),
        out_shape=[
            jax.ShapeDtypeStruct((PIECES, CP, PP), bf16),
            jax.ShapeDtypeStruct((2, CP, PP), bf16),
        ],
        compiler_params=params(),
        name="gather_field",
    )(pieces, recv)


def halo_kernel(field_ref, pack_ref, top_ref, bottom_ref, side_ref, send_sem, recv_sem):
    face = lax.axis_index("face")
    tile = lax.axis_index("tile")

    def at(df, dt):
        return (lax.rem(face + df + 4, 4), lax.rem(tile + dt + 32, 32))

    plan = [
        (field_ref.at[pl.ds(56, 8)], top_ref, at(0, 1)),
        (field_ref.at[pl.ds(0, 8)], bottom_ref, at(0, -1)),
    ]
    for dt in (-1, 0, 1):
        plan.append((pack_ref.at[1], side_ref.at[1 - dt], at(1, dt)))
        plan.append((pack_ref.at[0], side_ref.at[4 - dt], at(-1, dt)))
    barrier = pltpu.get_barrier_semaphore()
    for _, _, to in plan:
        pl.semaphore_signal(barrier, inc=1, device_id=to, device_id_type=MESH)
    pl.semaphore_wait(barrier, len(plan))
    copies = [
        pltpu.make_async_remote_copy(
            src_ref=src,
            dst_ref=dst,
            send_sem=send_sem.at[i],
            recv_sem=recv_sem.at[i],
            device_id=to,
            device_id_type=MESH,
        )
        for i, (src, dst, to) in enumerate(plan)
    ]
    for copy in copies:
        copy.start()
    for copy in copies:
        copy.wait()


def halo(field, pack):
    vmem = pl.BlockSpec(memory_space=pltpu.VMEM)
    return pl.pallas_call(
        halo_kernel,
        in_specs=[vmem, vmem],
        out_specs=[vmem, vmem, vmem],
        out_shape=[
            jax.ShapeDtypeStruct((8, CP, PP), bf16),
            jax.ShapeDtypeStruct((8, CP, PP), bf16),
            jax.ShapeDtypeStruct((6, CP, PP), bf16),
        ],
        scratch_shapes=[pltpu.SemaphoreType.DMA((8,)), pltpu.SemaphoreType.DMA((8,))],
        compiler_params=pltpu.CompilerParams(collective_id=0, has_side_effects=True),
        name="halo",
    )(field, pack)


def conv_kernel(
    meta_ref, field_ref, top_ref, bottom_ref, side_ref, wf_ref, wb_ref, cot_ref,
    act_ref, grad_ref, dfield_ref, x_ref, d_ref, pre_ref,
):
    step = pl.program_id(0)

    @pl.when(step == 0)
    def _():
        tile_at = meta_ref[0]
        has_top = (tile_at != 0).astype(f32)
        has_bottom = (tile_at != 31).astype(f32)
        lane = lax.broadcasted_iota(jnp.int32, (CP, PP), 1)

        def row(q, tiles, lefts, rights, at, factor):
            ext_l = pltpu.roll(lefts, (254 - 2 * at) % 128, 1) if 2 * at != 126 else lefts
            ext_r = pltpu.roll(rights, (128 - 2 * at) % 128, 1) if at else rights
            ext = jnp.where(lane < 2, ext_r, jnp.where(lane >= 126, ext_l, 0.0))
            full = jnp.concatenate(tiles + [ext], axis=1)
            if factor is not None:
                full = full * factor
            x_ref[q, 0:CP] = pltpu.roll(full, 1, 1).astype(bf16)
            x_ref[q, CP : 2 * CP] = full.astype(bf16)
            x_ref[q, 2 * CP : 3 * CP] = pltpu.roll(full, WIDE - 1, 1).astype(bf16)

        sides = [side_ref[i].astype(f32) for i in range(6)]
        for q in range(20):
            if q < 2:
                tiles = [top_ref[q * 4 + i].astype(f32) for i in range(4)]
                row(q, tiles, sides[0], sides[3], 14 + q, has_top)
            elif q < 18:
                tiles = [field_ref[(q - 2) * 4 + i].astype(f32) for i in range(4)]
                row(q, tiles, sides[1], sides[4], q - 2, None)
            else:
                tiles = [bottom_ref[(q - 18) * 4 + i].astype(f32) for i in range(4)]
                row(q, tiles, sides[2], sides[5], q - 18, has_bottom)
        grad_ref[...] = jnp.zeros_like(grad_ref)

    total = jnp.dot(wf_ref[0], x_ref[step], preferred_element_type=f32)
    total += jnp.dot(wf_ref[1], x_ref[step + 1], preferred_element_type=f32)
    total += jnp.dot(wf_ref[2], x_ref[step + 2], preferred_element_type=f32)
    pre_ref[...] = total
    for at in range(0, HID, 32):
        v = pre_ref[at : at + 32]
        square = v * v
        t = jnp.tanh(v * (0.7978845608 + (0.7978845608 * 0.044715) * square))
        half = 0.5 + 0.5 * t
        result = v * half
        slope = half + result * (1.0 - t) * (0.7978845608 + (0.7978845608 * 0.134145) * square)

        @pl.when((step >= 1) & (step <= ROWS))
        def _():
            act_ref[0, at : at + 32] = result[:, :COLS].astype(bf16)

        d_ref[step, at : at + 32] = (cot_ref[0, at : at + 32].astype(f32) * slope).astype(bf16)

    @pl.when((step >= 1) & (step <= ROWS))
    def _():
        dpre = d_ref[step][:, :COLS]
        for ky in range(3):
            grad_ref[ky] += lax.dot_general(
                x_ref[step + ky][:, :COLS], dpre, (((1,), (1,)), ((), ())),
                preferred_element_type=f32,
            )

    @pl.when(step >= 2)
    def _():
        back = jnp.dot(wb_ref[0], d_ref[step], preferred_element_type=f32)
        back += jnp.dot(wb_ref[1], d_ref[step - 1], preferred_element_type=f32)
        back += jnp.dot(wb_ref[2], d_ref[step - 2], preferred_element_type=f32)
        out = (
            pltpu.roll(back[0:CP], WIDE - 1, 1)
            + back[CP : 2 * CP]
            + pltpu.roll(back[2 * CP : 3 * CP], 1, 1)
        )
        for i in range(4):
            dfield_ref[i] = out[:, i * PP : (i + 1) * PP].astype(bf16)


def conv(meta, field, top, bottom, side, wf, wb, cot):
    return pl.pallas_call(
        conv_kernel,
        grid_spec=pltpu.PrefetchScalarGridSpec(
            num_scalar_prefetch=1,
            grid=(ROWS + 2,),
            in_specs=[
                whole(field.shape),
                whole(top.shape),
                whole(bottom.shape),
                whole(side.shape),
                whole(wf.shape),
                whole(wb.shape),
                pl.BlockSpec((1, HID, WIDE), lambda i, *a: (i, 0, 0)),
            ],
            out_specs=[
                pl.BlockSpec(
                    (1, HID, COLS), lambda i, *a: (jnp.clip(i - 1, 0, ROWS - 1), 0, 0)
                ),
                whole((3, 3 * CP, HID)),
                pl.BlockSpec((4, CP, PP), lambda i, *a: (jnp.maximum(i - 2, 0), 0, 0)),
            ],
            scratch_shapes=[
                pltpu.VMEM((20, 3 * CP, WIDE), bf16),
                pltpu.VMEM((ROWS + 2, HID, WIDE), bf16),
                pltpu.VMEM((HID, WIDE), f32),
            ],
        ),
        out_shape=[
            jax.ShapeDtypeStruct((ROWS, HID, COLS), bf16),
            jax.ShapeDtypeStruct((3, 3 * CP, HID), f32),
            jax.ShapeDtypeStruct((PIECES, CP, PP), bf16),
        ],
        compiler_params=params(),
        name="conv",
    )(meta, field, top, bottom, side, wf, wb, cot)


def reply_kernel(piece_ref, dfield_ref, out_ref):
    step = pl.program_id(0)
    for g in range(GRP):
        parts = []
        for s in range(2):
            piece = piece_ref[(step * GRP + g) * 2 + s]
            parts.append(dfield_ref[piece].astype(f32)[:SL])
        out_ref[g] = jnp.concatenate(parts, axis=0).astype(bf16)


def replies(pieces, dfield):
    return pl.pallas_call(
        reply_kernel,
        grid_spec=pltpu.PrefetchScalarGridSpec(
            num_scalar_prefetch=1,
            grid=(DEVS // GRP,),
            in_specs=[whole(dfield.shape)],
            out_specs=pl.BlockSpec((GRP, 2 * SL, PP), lambda i, *a: (i, 0, 0)),
        ),
        out_shape=jax.ShapeDtypeStruct((DEVS, 2 * SL, PP), bf16),
        compiler_params=params(),
        name="reply",
    )(pieces, dfield)


def final_kernel(place_ref, back_ref, w_ref, out_ref):
    step = pl.program_id(0)
    for g in range(4):
        total = jnp.zeros((SL, PP), f32)
        for j in range(K):
            code = place_ref[(step * 4 + g) * K + j]
            both = back_ref[code >> 2].astype(f32)
            got = jnp.where(((code >> 1) & 1) == 0, both[:SL], both[SL:])
            got = (got * (code & 1).astype(f32)).astype(bf16)
            total += lax.dot_general(
                got, w_ref[g, j], (((1,), (1,)), ((), ())), preferred_element_type=f32
            )
        out_ref[g] = total[:C].astype(bf16)


def final_products(places, back, weight):
    blocks = weight.shape[0]
    return pl.pallas_call(
        final_kernel,
        grid_spec=pltpu.PrefetchScalarGridSpec(
            num_scalar_prefetch=1,
            grid=(blocks // 4,),
            in_specs=[
                whole(back.shape),
                pl.BlockSpec((4, K, PP, PP), lambda i, *a: (i, 0, 0, 0)),
            ],
            out_specs=pl.BlockSpec((4, C, PP), lambda i, *a: (i, 0, 0)),
        ),
        out_shape=jax.ShapeDtypeStruct((blocks, C, PP), bf16),
        compiler_params=params(),
        name="final",
    )(places, back, weight)


def exchange(value):
    return lax.all_to_all(value, ("face", "tile"), split_axis=0, concat_axis=0, tiled=True)


def wide_cotangent(cot):
    up = [(i, i + 1) for i in range(31)]
    down = [(i + 1, i) for i in range(31)]
    cot = jnp.concatenate(
        [
            lax.ppermute(cot[:, ROWS - 1 :], "tile", up),
            cot,
            lax.ppermute(cot[:, :1], "tile", down),
        ],
        axis=1,
    )
    before = lax.ppermute(cot[:, :, COLS - 1 :], "face", [(i, (i + 1) % 4) for i in range(4)])
    after = lax.ppermute(cot[:, :, :1], "face", [((i + 1) % 4, i) for i in range(4)])
    gap = jnp.zeros((HID, ROWS + 2, WIDE - COLS - 2), bf16)
    return jnp.concatenate([cot, after, gap, before], axis=2).transpose(1, 0, 2)


def local(latlon, intersection_weight, target_dev, target_piece, counts, conv_weight, cotangent):
    blocks = latlon.shape[0]
    owners = jnp.arange(DEVS, dtype=jnp.int32)
    live = (jnp.arange(K, dtype=jnp.int32)[None, :] < counts[:, None]).astype(jnp.int32)
    entry = jnp.arange(blocks * K, dtype=jnp.int32).reshape(blocks, K)
    code = (entry * 64 + target_piece) * 2 + live
    mine = target_dev[None] == owners[:, None, None]
    first = jnp.min(jnp.where(mine, code[None], jnp.int32(1 << 24)), axis=(1, 2))
    second = jnp.max(jnp.where(mine, code[None], jnp.int32(-1)), axis=(1, 2))
    keys = jnp.stack([first, second], axis=1).reshape(-1)
    flat = target_dev.reshape(-1)
    order = entry.reshape(-1)
    slot = jnp.sum(
        ((flat[:, None] == flat[None, :]) & (order[None, :] < order[:, None])).astype(jnp.int32),
        axis=1,
    )
    places = flat * 4 + slot * 2 + live.reshape(-1)

    cot = wide_cotangent(cotangent[0])
    send = partial_products(
        keys, latlon, intersection_weight.reshape(blocks * K, PP, PP)
    )
    recv = exchange(send)
    pieces = jnp.stack([recv[:, C, 0], recv[:, SL + C, 0]], axis=1).reshape(-1).astype(jnp.int32)
    field, pack = gather_field(pieces, recv)
    top, bottom, side = halo(field, pack)

    kernel = conv_weight.reshape(3, 3, HID, C)
    kernel = jnp.pad(kernel, ((0, 0), (0, 0), (0, 0), (0, CP - C)))
    wf = kernel.transpose(0, 2, 1, 3).reshape(3, HID, 3 * CP)
    wb = kernel.transpose(0, 1, 3, 2).reshape(3, 3 * CP, HID)
    meta = lax.axis_index("tile").astype(jnp.int32).reshape(1)
    act, grad, dfield = conv(meta, field, top, bottom, side, wf, wb, cot)
    activation = act.transpose(1, 0, 2)[None]

    back = exchange(replies(pieces, dfield))
    shares = exchange(grad.reshape(DEVS, -1))
    share = jnp.sum(shares, axis=0) * (1.0 / math.sqrt(DEVS * ROWS * COLS))
    summed = exchange(jnp.broadcast_to(share[None], (DEVS, share.shape[0])))
    grad_conv = summed.reshape(9, CP, HID)[:, :C].transpose(0, 2, 1)
    grad_latlon = final_products(places, back, intersection_weight)
    return (activation, grad_conv, grad_latlon)


def solution(mesh):
    placed = (
        P(("face", "tile"), None, None),
        P(("face", "tile"), None, None, None),
        P(("face", "tile"), None),
        P(("face", "tile"), None),
        P(("face", "tile")),
        P(),
        P("face", None, "tile", None),
    )
    return jax.shard_map(
        local,
        mesh=mesh,
        in_specs=placed,
        out_specs=(P("face", None, "tile", None), P(), P(("face", "tile"), None, None)),
        check_vma=False,
    )
```

time: 560 us -> 306 us (0.55); the launches traced: 551 us -> 305 us
  waiting for transfers between devices: 236 us -> 107 us
  matrix products: 122 us -> 0 us
  Pallas kernels: 0 us -> 96.1 us
  local copies, waits for them, and re-layouts: 119 us -> 30.4 us
  blocking collectives: 0 us -> 28 us
  starting transfers between devices: 48.3 us -> 31 us
  between operations: 14.8 us -> 0.78 us
    psum x1 -> x0, waiting for transfers between devices: 170 us -> none  [local(): grad_sum = lax.psum(jnp.stack(terms), ('face', 'tile'))]
    dot_general x31 -> x0, matrix products: 122 us -> none  [the longest x9 67.2 us: local(): jnp.einsum('oc,crw->orw', conv_weight[k], field_pad[:, ky:ky + ROWS, kx:k...]
    pallas_call x0 -> x6, Pallas kernels: none -> 96.1 us  [the longest x1 36.1 us: conv(): pl.pallas_call(conv_kernel, grid_spec=pltpu.PrefetchScalarGridSpec(num_sc...]
    scatter x3 -> x0, local copies, waits for them, and re-layouts: 56.8 us -> none  [the longest x2 45.7 us: local(): send = jnp.zeros((devices, slots, C, PP), jnp.bfloat16).at[flat_dev, slot...]
    ppermute x8 -> x4, waiting for transfers between devices: 7.22 us -> 48.6 us  [the longest x1 36.3 us: wide_cotangent(): lax.ppermute(cot[:, :1], 'tile', down)]
    all_to_all x0 -> x1, blocking collectives: none -> 28 us  [exchange(): lax.all_to_all(value, ('face', 'tile'), split_axis=0, concat_axis=0, tile...]
    all_to_all x4 -> x1, local copies, waits for them, and re-layouts: 16.8 us -> 2.27 us  [exchange(): lax.all_to_all(value, ('face', 'tile'), split_axis=0, concat_axis=0, tile...]
    all_to_all x3, starting transfers between devices: 36.9 us -> 22.4 us  [exchange(): lax.all_to_all(value, ('face', 'tile'), split_axis=0, concat_axis=0, tile...]
  transfers between devices with their start and end apart: 12 -> 7, of which waited for: 7 -> 4; matrix products, arithmetic and copies ran while one was open for 16% -> 9% of each run, Pallas kernels for 0% -> 3%
where the time goes in v1:
time: 306 us; the launch traced here: 305 us
  waiting for transfers between devices  107 us (35%)
  Pallas kernels  96.1 us (31%)
  starting transfers between devices  31 us (10%)
  local copies, waits for them, and re-layouts  30.4 us (10%)
  blocking collectives  28 us (9%)
  other arithmetic  12.1 us (4%)
    all_to_all x3, waiting for transfers between devices, exchange(): lax.all_to_all(value, ('face', 'tile'), split_axis=0, concat_axis=0, tile...  58.1 us
    ppermute x1, waiting for transfers between devices, wide_cotangent(): lax.ppermute(cot[:, :1], 'tile', down)  36.3 us
    pallas_call x1, Pallas kernels, conv(): pl.pallas_call(conv_kernel, grid_spec=pltpu.PrefetchScalarGridSpec(num_sc...  36.1 us
    all_to_all x1, blocking collectives, exchange(): lax.all_to_all(value, ('face', 'tile'), split_axis=0, concat_axis=0, tile...  28 us
    all_to_all x3, starting transfers between devices, exchange(): lax.all_to_all(value, ('face', 'tile'), split_axis=0, concat_axis=0, tile...  22.4 us
    unnamed x13, local copies, waits for them, and re-layouts  17 us
    pallas_call x1, Pallas kernels, final_products(): pl.pallas_call(final_kernel, grid_spec=pltpu.PrefetchScalarGridSpec(num_s...  16.2 us
    pallas_call x1, Pallas kernels, partial_products(): pl.pallas_call(partial_kernel, grid_spec=pltpu.PrefetchScalarGridSpec(num...  13.3 us
  transfers between devices with their start and end apart: 7, of which 4 were waited for; matrix products, arithmetic and copies ran while one was open for 9% of the time, Pallas kernels for 3%

profile of v1, /device:TPU:1, one launch (start us, length us, event | category | flops | bytes accessed | tf_op | source)
XLA Modules:
  0.0 305.0 jit_solution(18244932849881055020)
XLA Ops:
  3.0 3.1 %copy.45.lat_ref = bf16[64,74,128]{2,1,0:T(8,128)(2,1)} copy(bf16[64,74,128]{2,0,1:T(8,128)(2,1)} %param.7) | data formatting | bytes 2424832 | tf_op args[0]
  6.1 13.3 %partial.1 = bf16[128,152,128]{2,1,0:T(8,128)(2,1)} custom-call(s32[256]{0:T(256)} %reshape.69.key_ref, bf16[64,74,128]{2,1,0:T(8,128)(2,1)} %copy.45.lat_ref, bf16[256,128,128]{2,1,0:T(8,128)(2,1)} %bitcast.26), custom_call_target="tpu_custom_call" | custom-call | tf_op jit(solution)/shard_map/partial/pallas_call | solution.py:53
  19.5 11.9 %all-to-all-start = ((bf16[128,152,128]{2,1,0:T(8,128)(2,1)}), bf16[128,152,128]{2,1,0:T(8,128)(2,1)}, u32[]{:S(2)}, u32[]{:S(2)}) async-start(bf16[128,152,128]{2,1,0:T(8,128)(2,1)} %partial.1), calls=%async_computation | async-start | bytes 9961472 | tf_op jit(solution)/shard_map/all_to_all | solution.py:346
  31.4 4.5 %copy.59 = bf16[1,256,16,512]{3,1,2,0:T(8,128)(2,1)S(1)} copy(bf16[1,256,16,512]{3,2,1,0:T(8,128)(2,1)} %param.13) | data formatting | bytes 8388608 | tf_op args[6]
  35.9 3.0 collective-permute-start.1
  39.0 2.5 collective-permute-start
  41.5 36.3 %collective-permute-done.1 = bf16[256,1,512]{2,0,1:T(8,128)(2,1)S(1)} collective-permute-done((bf16[256,1,512]{2,0,1:T(8,128)(2,1)S(1)}, bf16[256,1,512]{2,0,1:T(8,128)(2,1)S(1)}, u32[]{:S(2)}, u32[]{:S(2)}) %collective-permute-start.1) | collective-permute-done | bytes 262176 | tf_op jit(solution)/shard_map/ppermute | solution.py:356
  77.8 12.4 %collective-permute-done = bf16[256,1,512]{2,0,1:T(8,128)(2,1)S(1)} collective-permute-done((bf16[256,1,512]{2,0,1:T(8,128)(2,1)S(1)}, bf16[256,1,512]{2,0,1:T(8,128)(2,1)S(1)}, u32[]{:S(2)}, u32[]{:S(2)}) %collective-permute-start) | collective-permute-done | bytes 262176 | tf_op jit(solution)/shard_map/ppermute | solution.py:354
  91.3 1.9 collective-permute-start.3
  98.0 6.8 %maximum_bitcast_fusion.cot_ref = bf16[18,256,640]{2,1,0:T(8,128)(2,1)} fusion(bf16[256,18,1]{2,0,1:T(8,128)(2,1)S(1)} %copy.51, bf16[256,18,1]{2,0,1:T(8,128)(2,1)S(1)} %copy.50, bf16[256,1,512]{2,0,1:T(8,128)(2,1)S(1)} %collective-permute-done.1, bf16[256,16,512]{2,0,1:T(8,128)(2,1)} %bitcast.25, bf16[256,1,512]{2,0,1:T(8,128)(2,1)S(1)} %collective-permute-done, ...), kind=kLoop, calls=%fused_computation | loop fusion | flops 35389440 | bytes 10636544 | tf_op jit(solution)/shard_map/transpose | solution.py:363
  104.8 2.1 slice_reduce_fusion.1
  107.8 11.0 %gather_field.1 = (bf16[64,80,128]{2,1,0:T(8,128)(2,1)}, bf16[2,80,128]{2,1,0:T(8,128)(2,1)}) custom-call(s32[256]{0:T(256)} %reshape.76.piece_ref, bf16[128,152,128]{2,1,0:T(8,128)(2,1)} %all-to-all-done.recv_ref), custom_call_target="tpu_custom_call" | custom-call | tf_op jit(solution)/shard_map/gather_field/pallas_call | solution.py:100
  118.8 11.1 %halo.1 = (bf16[8,80,128]{2,1,0:T(8,128)(2,1)}, bf16[8,80,128]{2,1,0:T(8,128)(2,1)}, bf16[6,80,128]{2,1,0:T(8,128)(2,1)}) custom-call(bf16[64,80,128]{2,1,0:T(8,128)(2,1)} %get-tuple-element.11.field_ref, bf16[2,80,128]{2,1,0:T(8,128)(2,1)} %get-tuple-element.12.pack_ref), custom_call_target="tpu_custom_call" | custom-call | tf_op jit(solution)/shard_map/halo/pallas_call | solution.py:155
  129.9 36.1 %conv.1 = (bf16[16,256,512]{2,1,0:T(8,128)(2,1)}, f32[3,240,256]{2,1,0:T(8,128)}, bf16[64,80,128]{2,1,0:T(8,128)(2,1)}) custom-call(s32[1]{0:T(128)} %bitcast.meta_ref, bf16[64,80,128]{2,1,0:T(8,128)(2,1)} %get-tuple-element.11.field_ref, bf16[8,80,128]{2,1,0:T(8,128)(2,1)} %get-tuple-element.13.top_ref, bf16[8,80,128]{2,1,0:T(8,128)(2,1)} %get-tuple-element.14.bottom_ref, ...), custom_call_target="tpu_custom_call" | custom-call | tf_op jit(solution)/shard_map/conv/pallas_call | solution.py:249
  166.0 2.3 all_to_all.21
  168.3 28.0 %all_to_all.26 = f32[128,1,1440]{2,1,0:T(1,128)S(1)} all-to-all(f32[128,1,1440]{2,1,0:T(1,128)S(1)} %all_to_all.21), channel_id=1, replica_groups=mesh['face'=4,'tile'=32] {'face','tile'}, dimensions={0} | all-to-all | bytes 1474560 | tf_op jit(solution)/shard_map/all_to_all | solution.py:346
  198.0 4.7 %all-to-all-start.2 = ((f32[128,1,1440]{2,1,0:T(1,128)}), f32[128,1,1440]{2,1,0:T(1,128)S(1)}, u32[]{:S(2)}, u32[]{:S(2)}) async-start(f32[128,1,1440]{2,1,0:T(1,128)} %broadcast_in_dim.41), calls=%async_computation.2 | async-start | bytes 1572864 | tf_op jit(solution)/shard_map/all_to_all | solution.py:346
  202.8 8.3 %reply.1 = bf16[128,152,128]{2,1,0:T(8,128)(2,1)} custom-call(s32[256]{0:T(256)} %reshape.76.piece_ref, bf16[64,80,128]{2,1,0:T(8,128)(2,1)} %get-tuple-element.18.dfield_ref), custom_call_target="tpu_custom_call" | custom-call | tf_op jit(solution)/shard_map/reply/pallas_call | solution.py:297
  211.1 8.1 %all-to-all-done.2 = f32[128,1,1440]{2,1,0:T(1,128)S(1)} async-done(((f32[128,1,1440]{2,1,0:T(1,128)}), f32[128,1,1440]{2,1,0:T(1,128)S(1)}, u32[]{:S(2)}, u32[]{:S(2)}) %all-to-all-start.2) | async-done | bytes 737312 | tf_op jit(solution)/shard_map/all_to_all | solution.py:346
  219.1 5.8 %all-to-all-start.3 = ((bf16[128,152,128]{2,1,0:T(8,128)(2,1)}), bf16[128,152,128]{2,1,0:T(8,128)(2,1)}, u32[]{:S(2)}, u32[]{:S(2)}) async-start(bf16[128,152,128]{2,1,0:T(8,128)(2,1)} %reply.1), calls=%async_computation.3 | async-start | bytes 9961472 | tf_op jit(solution)/shard_map/all_to_all | solution.py:346
  226.2 6.5 %copy.56 = bf16[1,256,16,512]{3,2,1,0:T(8,128)(2,1)} copy(bf16[1,256,16,512]{3,1,2,0:T(8,128)(2,1)} %bitcast.27) | data formatting | bytes 8388608
  236.1 50.0 %all-to-all-done.3.back_ref = bf16[128,152,128]{2,1,0:T(8,128)(2,1)} async-done(((bf16[128,152,128]{2,1,0:T(8,128)(2,1)}), bf16[128,152,128]{2,1,0:T(8,128)(2,1)}, u32[]{:S(2)}, u32[]{:S(2)}) %all-to-all-start.3) | async-done | bytes 4980768 | tf_op jit(solution)/shard_map/all_to_all | solution.py:346
  286.1 16.2 %final.1 = bf16[64,74,128]{2,1,0:T(8,128)(2,1)} custom-call(s32[256]{0:T(256)} %add_add_fusion.place_ref, bf16[128,152,128]{2,1,0:T(8,128)(2,1)} %all-to-all-done.3.back_ref, bf16[64,4,128,128]{3,2,1,0:T(8,128)(2,1)} %w_ref.1), custom_call_target="tpu_custom_call" | custom-call | tf_op jit(solution)/shard_map/final/pallas_call | solution.py:328
  302.3 2.7 copy.57
  (43 shorter events, 15.5 us)
Async XLA Ops:
  19.5 85.4 %all-to-all-start = ((bf16[128,152,128]{2,1,0:T(8,128)(2,1)}), bf16[128,152,128]{2,1,0:T(8,128)(2,1)}, u32[]{:S(2)}, u32[]{:S(2)}) async-start(bf16[128,152,128]{2,1,0:T(8,128)(2,1)} %partial.1), calls=%async_computation | async-start | bytes 9961472 | tf_op jit(solution)/shard_map/all_to_all | solution.py:346
  35.9 54.3 %copy-start = (bf16[1,256,16,512]{3,1,2,0:T(8,128)(2,1)}, bf16[1,256,16,512]{3,1,2,0:T(8,128)(2,1)S(1)}, u32[]{:S(2)}) copy-start(bf16[1,256,16,512]{3,1,2,0:T(8,128)(2,1)S(1)} %copy.59) | copy-start | bytes 12582916
  35.9 41.8 %collective-permute-start.1 = (bf16[256,1,512]{2,0,1:T(8,128)(2,1)S(1)}, bf16[256,1,512]{2,0,1:T(8,128)(2,1)S(1)}, u32[]{:S(2)}, u32[]{:S(2)}) collective-permute-start(bf16[256,1,512]{2,0,1:T(8,128)(2,1)S(1)} %get-tuple-element.38), channel_id=1, source_target_pairs={{1,0},{2,1},{3,2},{4,3},{5,4},{6,5},{7,6},{8,7},{9,8},{10,9},{11,1... | collective-permute-start | bytes 786440 | tf_op jit(solution)/shard_map/ppermute | solution.py:356
  39.0 51.2 %collective-permute-start = (bf16[256,1,512]{2,0,1:T(8,128)(2,1)S(1)}, bf16[256,1,512]{2,0,1:T(8,128)(2,1)S(1)}, u32[]{:S(2)}, u32[]{:S(2)}) collective-permute-start(bf16[256,1,512]{2,0,1:T(8,128)(2,1)S(1)} %get-tuple-element.37), channel_id=1, source_target_pairs={{0,1},{1,2},{2,3},{3,4},{4,5},{5,6},{6,7},{7,8},{8,9},{9,10},{10,1... | collective-permute-start | bytes 786440 | tf_op jit(solution)/shard_map/ppermute | solution.py:354
  91.3 5.5 %collective-permute-start.3 = (bf16[256,18,1]{0,1,2:T(8,128)(2,1)S(1)}, bf16[256,18,1]{0,1,2:T(8,128)(2,1)S(1)}, u32[]{:S(2)}, u32[]{:S(2)}) collective-permute-start(bf16[256,18,1]{0,1,2:T(8,128)(2,1)S(1)} %copy.49), channel_id=1, source_target_pairs={{0,32},{32,64},{64,96},{96,0},{1,33},{33,65},{65,97},{97,1},{2,34}... | collective-permute-start | bytes 27656 | tf_op jit(solution)/shard_map/ppermute | solution.py:360
  93.8 3.7 %collective-permute-start.2 = (bf16[256,18,1]{0,1,2:T(8,128)(2,1)S(1)}, bf16[256,18,1]{0,1,2:T(8,128)(2,1)S(1)}, u32[]{:S(2)}, u32[]{:S(2)}) collective-permute-start(bf16[256,18,1]{0,1,2:T(8,128)(2,1)S(1)} %copy.48), channel_id=1, source_target_pairs={{32,0},{64,32},{96,64},{0,96},{33,1},{65,33},{97,65},{1,97},{34,2}... | collective-permute-start | bytes 27656 | tf_op jit(solution)/shard_map/ppermute | solution.py:361
  95.8 9.0 %copy-start.1 = (bf16[3,3,256,80]{2,3,1,0:T(8,128)(2,1)}, bf16[3,3,256,80]{2,3,1,0:T(8,128)(2,1)S(1)}, u32[]{:S(2)}) copy-start(bf16[3,3,256,80]{2,3,1,0:T(8,128)(2,1)S(1)} %pad.4) | copy-start | bytes 1105924
  198.0 21.1 %all-to-all-start.2 = ((f32[128,1,1440]{2,1,0:T(1,128)}), f32[128,1,1440]{2,1,0:T(1,128)S(1)}, u32[]{:S(2)}, u32[]{:S(2)}) async-start(f32[128,1,1440]{2,1,0:T(1,128)} %broadcast_in_dim.41), calls=%async_computation.2 | async-start | bytes 1572864 | tf_op jit(solution)/shard_map/all_to_all | solution.py:346
  211.1 13.9 %copy-start.2 = (s32[64,4]{0,1:T(4,128)S(1)}, s32[64,4]{0,1:T(4,128)}, u32[]{:S(2)}) copy-start(s32[64,4]{0,1:T(4,128)} %param.9) | copy-start | bytes 3076
  211.1 14.0 %copy-start.3 = (s32[64]{0:T(128)S(1)}, s32[64]{0:T(128)}, u32[]{:S(2)}) copy-start(s32[64]{0:T(128)} %param.11) | copy-start | bytes 772
  219.1 67.0 %all-to-all-start.3 = ((bf16[128,152,128]{2,1,0:T(8,128)(2,1)}), bf16[128,152,128]{2,1,0:T(8,128)(2,1)}, u32[]{:S(2)}, u32[]{:S(2)}) async-start(bf16[128,152,128]{2,1,0:T(8,128)(2,1)} %reply.1), calls=%async_computation.3 | async-start | bytes 9961472 | tf_op jit(solution)/shard_map/all_to_all | solution.py:346

commit v2 on v1

--- a/solution.py
+++ b/solution.py
@@ -20,6 +20,8 @@
 PIECES = 64
 DEVS = 128
 GRP = 8
+SHARE = 11
+BACK = 160
 VMEM_LIMIT = 63 * 1024 * 1024
 MESH = pl.DeviceIdType.MESH
 f32 = jnp.float32
@@ -60,6 +62,9 @@
         ),
         out_shape=jax.ShapeDtypeStruct((DEVS, 2 * SL, PP), bf16),
         compiler_params=params(),
+        cost_estimate=pl.CostEstimate(
+            flops=1_300_000_000, bytes_accessed=15_000_000, transcendentals=0
+        ),
         name="partial",
     )(keys, lat, weight)
 
@@ -168,8 +173,8 @@
 
 
 def conv_kernel(
-    meta_ref, field_ref, top_ref, bottom_ref, side_ref, wf_ref, wb_ref, cot_ref,
-    act_ref, grad_ref, dfield_ref, x_ref, d_ref, pre_ref,
+    meta_ref, field_ref, top_ref, bottom_ref, side_ref, wf_ref, wb_ref, cot_ref, rim_ref, edge_ref,
+    act_ref, rows_ref, dfield_ref, x_ref, d_ref, pre_ref, grad_ref,
 ):
     step = pl.program_id(0)
 
@@ -220,7 +225,11 @@
         def _():
             act_ref[0, at : at + 32] = result[:, :COLS].astype(bf16)
 
-        d_ref[step, at : at + 32] = (cot_ref[0, at : at + 32].astype(f32) * slope).astype(bf16)
+        inner = (step >= 1) & (step <= ROWS)
+        cot = jnp.where(inner, cot_ref[0, at : at + 32], rim_ref[0, at : at + 32]).astype(f32)
+        edge = edge_ref[0, at : at + 32].astype(f32)
+        d_ref[step, at : at + 32, :COLS] = (cot * slope[:, :COLS]).astype(bf16)
+        d_ref[step, at : at + 32, COLS:] = (edge * slope[:, COLS:]).astype(bf16)
 
     @pl.when((step >= 1) & (step <= ROWS))
     def _():
@@ -244,8 +253,20 @@
         for i in range(4):
             dfield_ref[i] = out[:, i * PP : (i + 1) * PP].astype(bf16)
 
-
-def conv(meta, field, top, bottom, side, wf, wb, cot):
+    @pl.when(step == pl.num_programs(0) - 1)
+    def _():
+        for h in range(2):
+            for k in range(9):
+                at = (k % 3) * CP
+                rows_ref[pl.ds((h * 9 + k) * C, C)] = grad_ref[
+                    k // 3, at : at + C, h * PP : (h + 1) * PP
+                ]
+        rows_ref[pl.ds(18 * C, DEVS * SHARE - 18 * C)] = jnp.zeros(
+            (DEVS * SHARE - 18 * C, PP), f32
+        )
+
+
+def conv(meta, field, top, bottom, side, wf, wb, cots):
     return pl.pallas_call(
         conv_kernel,
         grid_spec=pltpu.PrefetchScalarGridSpec(
@@ -258,69 +279,116 @@
                 whole(side.shape),
                 whole(wf.shape),
                 whole(wb.shape),
-                pl.BlockSpec((1, HID, WIDE), lambda i, *a: (i, 0, 0)),
+                pl.BlockSpec(
+                    (1, HID, COLS), lambda i, *a: (jnp.clip(i - 1, 0, ROWS - 1), 0, 0)
+                ),
+                pl.BlockSpec((1, HID, COLS), lambda i, *a: (jnp.minimum(i, 1), 0, 0)),
+                pl.BlockSpec((1, HID, PP), lambda i, *a: (i, 0, 0)),
             ],
             out_specs=[
                 pl.BlockSpec(
                     (1, HID, COLS), lambda i, *a: (jnp.clip(i - 1, 0, ROWS - 1), 0, 0)
                 ),
-                whole((3, 3 * CP, HID)),
+                whole((DEVS * SHARE, PP)),
                 pl.BlockSpec((4, CP, PP), lambda i, *a: (jnp.maximum(i - 2, 0), 0, 0)),
             ],
             scratch_shapes=[
                 pltpu.VMEM((20, 3 * CP, WIDE), bf16),
                 pltpu.VMEM((ROWS + 2, HID, WIDE), bf16),
                 pltpu.VMEM((HID, WIDE), f32),
+                pltpu.VMEM((3, 3 * CP, HID), f32),
             ],
         ),
         out_shape=[
             jax.ShapeDtypeStruct((ROWS, HID, COLS), bf16),
-            jax.ShapeDtypeStruct((3, 3 * CP, HID), f32),
+            jax.ShapeDtypeStruct((DEVS * SHARE, PP), f32),
             jax.ShapeDtypeStruct((PIECES, CP, PP), bf16),
         ],
         compiler_params=params(),
         name="conv",
-    )(meta, field, top, bottom, side, wf, wb, cot)
-
-
-def reply_kernel(piece_ref, dfield_ref, out_ref):
+    )(meta, field, top, bottom, side, wf, wb, *cots)
+
+
+def channel_major_kernel(in_ref, out_ref, turn_ref):
+    for i in range(COLS // PP):
+        for r in range(ROWS):
+            turn_ref[i, pl.ds(r, 32, stride=ROWS), :] = in_ref[
+                r, :, i * PP : (i + 1) * PP
+            ].astype(f32)
+    for i in range(COLS // PP):
+        for o in range(32):
+            out_ref[o, :, i * PP : (i + 1) * PP] = turn_ref[
+                i, o * ROWS : (o + 1) * ROWS
+            ].astype(bf16)
+
+
+def channel_major(act):
+    return pl.pallas_call(
+        channel_major_kernel,
+        grid=(HID // 32,),
+        in_specs=[pl.BlockSpec((ROWS, 32, COLS), lambda i: (0, i, 0))],
+        out_specs=pl.BlockSpec((32, ROWS, COLS), lambda i: (i, 0, 0)),
+        out_shape=jax.ShapeDtypeStruct((HID, ROWS, COLS), bf16),
+        scratch_shapes=[pltpu.VMEM((COLS // PP, 32 * ROWS, PP), f32)],
+        compiler_params=params(),
+        cost_estimate=pl.CostEstimate(
+            flops=20_000_000, bytes_accessed=160_000_000, transcendentals=0
+        ),
+        name="channel_major",
+    )(act)
+
+
+def reply_kernel(piece_ref, dfield_ref, rows_ref, out_ref):
     step = pl.program_id(0)
+    terms = rows_ref[...]
     for g in range(GRP):
         parts = []
         for s in range(2):
             piece = piece_ref[(step * GRP + g) * 2 + s]
-            parts.append(dfield_ref[piece].astype(f32)[:SL])
+            parts.append(dfield_ref[piece].astype(f32)[:C])
+        parts.append(terms[g * SHARE : (g + 1) * SHARE])
+        parts.append(jnp.zeros((BACK - 2 * C - SHARE, PP), f32))
         out_ref[g] = jnp.concatenate(parts, axis=0).astype(bf16)
 
 
-def replies(pieces, dfield):
+def replies(pieces, dfield, rows):
     return pl.pallas_call(
         reply_kernel,
         grid_spec=pltpu.PrefetchScalarGridSpec(
             num_scalar_prefetch=1,
             grid=(DEVS // GRP,),
-            in_specs=[whole(dfield.shape)],
-            out_specs=pl.BlockSpec((GRP, 2 * SL, PP), lambda i, *a: (i, 0, 0)),
-        ),
-        out_shape=jax.ShapeDtypeStruct((DEVS, 2 * SL, PP), bf16),
+            in_specs=[
+                whole(dfield.shape),
+                pl.BlockSpec((GRP * SHARE, PP), lambda i, *a: (i, 0)),
+            ],
+            out_specs=pl.BlockSpec((GRP, BACK, PP), lambda i, *a: (i, 0, 0)),
+        ),
+        out_shape=jax.ShapeDtypeStruct((DEVS, BACK, PP), bf16),
         compiler_params=params(),
         name="reply",
-    )(pieces, dfield)
-
-
-def final_kernel(place_ref, back_ref, w_ref, out_ref):
+    )(pieces, dfield, rows)
+
+
+def final_kernel(place_ref, back_hbm, w_ref, out_ref, back_ref, sem):
     step = pl.program_id(0)
+
+    @pl.when(step == 0)
+    def _():
+        copy = pltpu.make_async_copy(back_hbm, back_ref, sem)
+        copy.start()
+        copy.wait()
+
     for g in range(4):
-        total = jnp.zeros((SL, PP), f32)
+        total = jnp.zeros((C, PP), f32)
         for j in range(K):
             code = place_ref[(step * 4 + g) * K + j]
             both = back_ref[code >> 2].astype(f32)
-            got = jnp.where(((code >> 1) & 1) == 0, both[:SL], both[SL:])
+            got = jnp.where(((code >> 1) & 1) == 0, both[:C], both[C : 2 * C])
             got = (got * (code & 1).astype(f32)).astype(bf16)
             total += lax.dot_general(
                 got, w_ref[g, j], (((1,), (1,)), ((), ())), preferred_element_type=f32
             )
-        out_ref[g] = total[:C].astype(bf16)
+        out_ref[g] = total.astype(bf16)
 
 
 def final_products(places, back, weight):
@@ -331,13 +399,17 @@
             num_scalar_prefetch=1,
             grid=(blocks // 4,),
             in_specs=[
-                whole(back.shape),
+                pl.BlockSpec(memory_space=pltpu.HBM),
                 pl.BlockSpec((4, K, PP, PP), lambda i, *a: (i, 0, 0, 0)),
             ],
             out_specs=pl.BlockSpec((4, C, PP), lambda i, *a: (i, 0, 0)),
+            scratch_shapes=[pltpu.VMEM(back.shape, bf16), pltpu.SemaphoreType.DMA],
         ),
         out_shape=jax.ShapeDtypeStruct((blocks, C, PP), bf16),
         compiler_params=params(),
+        cost_estimate=pl.CostEstimate(
+            flops=1_300_000_000, bytes_accessed=30_000_000, transcendentals=0
+        ),
         name="final",
     )(places, back, weight)
 
@@ -346,21 +418,19 @@
     return lax.all_to_all(value, ("face", "tile"), split_axis=0, concat_axis=0, tiled=True)
 
 
-def wide_cotangent(cot):
+def cotangent_rim(cot):
     up = [(i, i + 1) for i in range(31)]
     down = [(i + 1, i) for i in range(31)]
-    cot = jnp.concatenate(
-        [
-            lax.ppermute(cot[:, ROWS - 1 :], "tile", up),
-            cot,
-            lax.ppermute(cot[:, :1], "tile", down),
-        ],
-        axis=1,
-    )
-    before = lax.ppermute(cot[:, :, COLS - 1 :], "face", [(i, (i + 1) % 4) for i in range(4)])
-    after = lax.ppermute(cot[:, :, :1], "face", [((i + 1) % 4, i) for i in range(4)])
-    gap = jnp.zeros((HID, ROWS + 2, WIDE - COLS - 2), bf16)
-    return jnp.concatenate([cot, after, gap, before], axis=2).transpose(1, 0, 2)
+    above = lax.ppermute(cot[:, ROWS - 1 :], "tile", up)
+    below = lax.ppermute(cot[:, :1], "tile", down)
+    ends = jnp.concatenate([above, cot, below], axis=1)
+    last, first = ends[:, :, COLS - 1 :], ends[:, :, :1]
+    before = lax.ppermute(last, "face", [(i, (i + 1) % 4) for i in range(4)])
+    after = lax.ppermute(first, "face", [((i + 1) % 4, i) for i in range(4)])
+    gap = jnp.zeros((HID, ROWS + 2, PP - 2), bf16)
+    side = jnp.concatenate([after, gap, before], axis=2).transpose(1, 0, 2)
+    rim = jnp.concatenate([above, below], axis=1).transpose(1, 0, 2)
+    return cot.transpose(1, 0, 2), rim, side
 
 
 def local(latlon, intersection_weight, target_dev, target_piece, counts, conv_weight, cotangent):
@@ -381,7 +451,7 @@
     )
     places = flat * 4 + slot * 2 + live.reshape(-1)
 
-    cot = wide_cotangent(cotangent[0])
+    cots = cotangent_rim(cotangent[0])
     send = partial_products(
         keys, latlon, intersection_weight.reshape(blocks * K, PP, PP)
     )
@@ -395,14 +465,15 @@
     wf = kernel.transpose(0, 2, 1, 3).reshape(3, HID, 3 * CP)
     wb = kernel.transpose(0, 1, 3, 2).reshape(3, 3 * CP, HID)
     meta = lax.axis_index("tile").astype(jnp.int32).reshape(1)
-    act, grad, dfield = conv(meta, field, top, bottom, side, wf, wb, cot)
-    activation = act.transpose(1, 0, 2)[None]
-
-    back = exchange(replies(pieces, dfield))
-    shares = exchange(grad.reshape(DEVS, -1))
-    share = jnp.sum(shares, axis=0) * (1.0 / math.sqrt(DEVS * ROWS * COLS))
-    summed = exchange(jnp.broadcast_to(share[None], (DEVS, share.shape[0])))
-    grad_conv = summed.reshape(9, CP, HID)[:, :C].transpose(0, 2, 1)
+    act, rows, dfield = conv(meta, field, top, bottom, side, wf, wb, cots)
+    activation = channel_major(act)[None]
+
+    back = exchange(replies(pieces, dfield, rows))
+    share = jnp.sum(back[:, 2 * C : 2 * C + SHARE].astype(f32), axis=0)
+    share = (share * (1.0 / math.sqrt(DEVS * ROWS * COLS))).astype(bf16)
+    summed = exchange(jnp.broadcast_to(share[None], (DEVS, SHARE, PP)))
+    summed = summed.reshape(DEVS * SHARE, PP)[: 18 * C].reshape(2, 9, C, PP)
+    grad_conv = summed.astype(f32).transpose(1, 0, 3, 2).reshape(9, HID, C)
     grad_latlon = final_products(places, back, intersection_weight)
     return (activation, grad_conv, grad_latlon)
 

time: 306 us -> 294 us (0.961)
  blocking collectives: 28 us -> 0 us
  Pallas kernels: 96.1 us -> 110 us
  starting transfers between devices: 31 us -> 41.1 us
  local copies, waits for them, and re-layouts: 30.4 us -> 22.6 us
  other arithmetic: 12.1 us -> 8.24 us
    all_to_all x1 -> x0, blocking collectives: 28 us -> none  [exchange(): lax.all_to_all(value, ('face', 'tile'), split_axis=0, concat_axis=0, tile...]
    all_to_all x3, starting transfers between devices: 22.4 us -> 32.6 us  [exchange(): lax.all_to_all(value, ('face', 'tile'), split_axis=0, concat_axis=0, tile...]
    pallas_call x0 -> x1, Pallas kernels: none -> 8.45 us  [channel_major(): pl.pallas_call(channel_major_kernel, grid=(HID // 32,), in_specs=[pl.Bloc...]
    all_to_all x3, waiting for transfers between devices: 58.1 us -> 63.6 us  [exchange(): lax.all_to_all(value, ('face', 'tile'), split_axis=0, concat_axis=0, tile...]
    unnamed x13 -> x14, local copies, waits for them, and re-layouts: 17 us -> 12.5 us
    transpose x1 -> x2, other arithmetic: 6.82 us -> 2.56 us  [the longest x1 1.74 us: cotangent_rim(): side = jnp.concatenate([after, gap, before], axis=2).transpose(1, 0, 2)]
  transfers between devices with their start and end apart: 7 -> 7, of which waited for: 4 -> 4; matrix products, arithmetic and copies ran while one was open for 9% -> 6% of each run, Pallas kernels for 3% -> 9%
where the time goes in v2:
time: 294 us; the launch traced here: 292 us
  Pallas kernels  110 us (37%)
  waiting for transfers between devices  109 us (37%)
  starting transfers between devices  41.1 us (14%)
  local copies, waits for them, and re-layouts  22.6 us (8%)
  other arithmetic  8.24 us (3%)
    all_to_all x3, waiting for transfers between devices, exchange(): lax.all_to_all(value, ('face', 'tile'), split_axis=0, concat_axis=0, tile...  63.6 us
    pallas_call x1, Pallas kernels, conv(): pl.pallas_call(conv_kernel, grid_spec=pltpu.PrefetchScalarGridSpec(num_sc...  37.1 us
    ppermute x1, waiting for transfers between devices, cotangent_rim(): below = lax.ppermute(cot[:, :1], 'tile', down)  33.1 us
    all_to_all x3, starting transfers between devices, exchange(): lax.all_to_all(value, ('face', 'tile'), split_axis=0, concat_axis=0, tile...  32.6 us
    pallas_call x1, Pallas kernels, final_products(): pl.pallas_call(final_kernel, grid_spec=pltpu.PrefetchScalarGridSpec(num_s...  17.2 us
    pallas_call x1, Pallas kernels, partial_products(): pl.pallas_call(partial_kernel, grid_spec=pltpu.PrefetchScalarGridSpec(num...  13.4 us
    unnamed x14, local copies, waits for them, and re-layouts  12.5 us
    ppermute x1, waiting for transfers between devices, cotangent_rim(): above = lax.ppermute(cot[:, ROWS - 1:], 'tile', up)  12.4 us
  transfers between devices with their start and end apart: 7, of which 4 were waited for; matrix products, arithmetic and copies ran while one was open for 6% of the time, Pallas kernels for 9%

profile of v2, /device:TPU:1, one launch (start us, length us, event | category | flops | bytes accessed | tf_op | source)
XLA Modules:
  0.0 291.9 jit_solution(6165097388003645352)
XLA Ops:
  3.0 3.1 %copy.53.lat_ref = bf16[64,74,128]{2,1,0:T(8,128)(2,1)} copy(bf16[64,74,128]{2,0,1:T(8,128)(2,1)} %param.7) | data formatting | bytes 2424832 | tf_op args[0]
  6.1 13.4 %partial.1 = bf16[128,152,128]{2,1,0:T(8,128)(2,1)} custom-call(s32[256]{0:T(256)} %reshape.68.key_ref, bf16[64,74,128]{2,1,0:T(8,128)(2,1)} %copy.53.lat_ref, bf16[256,128,128]{2,1,0:T(8,128)(2,1)} %bitcast.30), custom_call_target="tpu_custom_call" | custom-call | flops 1300000000 | bytes 15000000 | tf_op jit(solution)/shard_map/partial/pallas_call | solution.py:55
  19.5 11.9 %all-to-all-start = ((bf16[128,152,128]{2,1,0:T(8,128)(2,1)}), bf16[128,152,128]{2,1,0:T(8,128)(2,1)}, u32[]{:S(2)}, u32[]{:S(2)}) async-start(bf16[128,152,128]{2,1,0:T(8,128)(2,1)} %partial.1), calls=%async_computation | async-start | bytes 9961472 | tf_op jit(solution)/shard_map/all_to_all | solution.py:418
  31.4 4.6 %copy.67 = bf16[1,256,16,512]{3,1,2,0:T(8,128)(2,1)S(1)} copy(bf16[1,256,16,512]{3,2,1,0:T(8,128)(2,1)} %param.13) | data formatting | bytes 8388608 | tf_op args[6]
  36.0 2.0 copy-done
  38.1 3.0 %collective-permute-start.1 = (bf16[256,1,512]{2,0,1:T(8,128)(2,1)S(1)}, bf16[256,1,512]{2,0,1:T(8,128)(2,1)S(1)}, u32[]{:S(2)}, u32[]{:S(2)}) collective-permute-start(bf16[256,1,512]{2,0,1:T(8,128)(2,1)S(1)} %get-tuple-element.41), channel_id=1, source_target_pairs={{1,0},{2,1},{3,2},{4,3},{5,4},{6,5},{7,6},{8,7},{9,8},{10,9},{11,1... | collective-permute-start | bytes 786440 | tf_op jit(solution)/shard_map/ppermute | solution.py:425
  41.1 2.5 collective-permute-start
  44.7 33.1 %collective-permute-done.1 = bf16[256,1,512]{2,0,1:T(8,128)(2,1)S(1)} collective-permute-done((bf16[256,1,512]{2,0,1:T(8,128)(2,1)S(1)}, bf16[256,1,512]{2,0,1:T(8,128)(2,1)S(1)}, u32[]{:S(2)}, u32[]{:S(2)}) %collective-permute-start.1) | collective-permute-done | bytes 262176 | tf_op jit(solution)/shard_map/ppermute | solution.py:425
  77.8 12.4 %collective-permute-done = bf16[256,1,512]{2,0,1:T(8,128)(2,1)S(1)} collective-permute-done((bf16[256,1,512]{2,0,1:T(8,128)(2,1)S(1)}, bf16[256,1,512]{2,0,1:T(8,128)(2,1)S(1)}, u32[]{:S(2)}, u32[]{:S(2)}) %collective-permute-start) | collective-permute-done | bytes 262176 | tf_op jit(solution)/shard_map/ppermute | solution.py:424
  90.2 2.0 pad_maximum_fusion.2
  92.8 1.9 collective-permute-start.3
  98.6 1.7 maximum_bitcast_fusion.edge_ref
  100.3 2.1 slice_reduce_fusion.1
  103.2 11.0 %gather_field.1 = (bf16[64,80,128]{2,1,0:T(8,128)(2,1)}, bf16[2,80,128]{2,1,0:T(8,128)(2,1)}) custom-call(s32[256]{0:T(256)} %reshape.77.piece_ref, bf16[128,152,128]{2,1,0:T(8,128)(2,1)} %all-to-all-done.recv_ref), custom_call_target="tpu_custom_call" | custom-call | tf_op jit(solution)/shard_map/gather_field/pallas_call | solution.py:105
  114.2 11.8 %halo.1 = (bf16[8,80,128]{2,1,0:T(8,128)(2,1)}, bf16[8,80,128]{2,1,0:T(8,128)(2,1)}, bf16[6,80,128]{2,1,0:T(8,128)(2,1)}) custom-call(bf16[64,80,128]{2,1,0:T(8,128)(2,1)} %get-tuple-element.11.field_ref, bf16[2,80,128]{2,1,0:T(8,128)(2,1)} %get-tuple-element.12.pack_ref), custom_call_target="tpu_custom_call" | custom-call | tf_op jit(solution)/shard_map/halo/pallas_call | solution.py:160
  126.1 37.1 %conv.1 = (bf16[16,256,512]{2,1,0:T(8,128)(2,1)}, f32[1408,128]{1,0:T(8,128)}, bf16[64,80,128]{2,1,0:T(8,128)(2,1)}) custom-call(s32[1]{0:T(128)} %bitcast.meta_ref, bf16[64,80,128]{2,1,0:T(8,128)(2,1)} %get-tuple-element.11.field_ref, bf16[8,80,128]{2,1,0:T(8,128)(2,1)} %get-tuple-element.13.top_ref, bf16[8,80,128]{2,1,0:T(8,128)(2,1)} %get-tuple-element.14.bottom_ref, ...), custom_call_target="tpu_custom_call" | custom-call | tf_op jit(solution)/shard_map/conv/pallas_call | solution.py:270
  163.2 10.8 %reply.1 = bf16[128,160,128]{2,1,0:T(8,128)(2,1)} custom-call(s32[256]{0:T(256)} %reshape.77.piece_ref, bf16[64,80,128]{2,1,0:T(8,128)(2,1)} %get-tuple-element.17.dfield_ref, f32[1408,128]{1,0:T(8,128)} %get-tuple-element.18.rows_ref), custom_call_target="tpu_custom_call" | custom-call | tf_op jit(solution)/shard_map/reply/pallas_call | solution.py:355
  173.9 12.7 %all-to-all-start.1 = ((bf16[128,160,128]{2,1,0:T(8,128)(2,1)}), bf16[128,160,128]{2,1,0:T(8,128)(2,1)}, u32[]{:S(2)}, u32[]{:S(2)}) async-start(bf16[128,160,128]{2,1,0:T(8,128)(2,1)} %reply.1), calls=%async_computation.1 | async-start | bytes 10485760 | tf_op jit(solution)/shard_map/all_to_all | solution.py:418
  186.9 63.6 %all-to-all-done.1.back_hbm = bf16[128,160,128]{2,1,0:T(8,128)(2,1)} async-done(((bf16[128,160,128]{2,1,0:T(8,128)(2,1)}), bf16[128,160,128]{2,1,0:T(8,128)(2,1)}, u32[]{:S(2)}, u32[]{:S(2)}) %all-to-all-start.1) | async-done | bytes 5242912 | tf_op jit(solution)/shard_map/all_to_all | solution.py:418
  252.6 8.0 %all-to-all-start.2 = ((bf16[128,11,128]{2,1,0:T(8,128)(2,1)}), bf16[128,11,128]{2,1,0:T(8,128)(2,1)S(1)}, u32[]{:S(2)}, u32[]{:S(2)}) async-start(bf16[128,11,128]{2,1,0:T(8,128)(2,1)} %broadcast_in_dim.41), calls=%async_computation.2 | async-start | bytes 1048576 | tf_op jit(solution)/shard_map/all_to_all | solution.py:418
  261.6 8.4 %channel_major.1 = bf16[256,16,512]{2,1,0:T(8,128)(2,1)} custom-call(bf16[16,256,512]{2,1,0:T(8,128)(2,1)} %get-tuple-element.16.in_ref), custom_call_target="tpu_custom_call" | custom-call | flops 20000000 | bytes 160000000 | tf_op jit(solution)/shard_map/channel_major/pallas_call | solution.py:326
  270.0 17.2 %final.1 = bf16[64,74,128]{2,1,0:T(8,128)(2,1)} custom-call(s32[256]{0:T(256)} %add_add_fusion.place_ref, bf16[128,160,128]{2,1,0:T(8,128)(2,1)} %all-to-all-done.1.back_hbm, bf16[64,4,128,128]{3,2,1,0:T(8,128)(2,1)} %w_ref.1), custom_call_target="tpu_custom_call" | custom-call | flops 1300000000 | bytes 30000000 | tf_op jit(solution)/shard_map/final/pallas_call | solution.py:396
  287.2 2.7 copy.64
  290.5 1.4 reshape.79
  (46 shorter events, 12.6 us)
Async XLA Ops:
  19.5 80.8 %all-to-all-start = ((bf16[128,152,128]{2,1,0:T(8,128)(2,1)}), bf16[128,152,128]{2,1,0:T(8,128)(2,1)}, u32[]{:S(2)}, u32[]{:S(2)}) async-start(bf16[128,152,128]{2,1,0:T(8,128)(2,1)} %partial.1), calls=%async_computation | async-start | bytes 9961472 | tf_op jit(solution)/shard_map/all_to_all | solution.py:418
  31.4 12.3 %copy-start.2 = (bf16[9,256,74]{1,2,0:T(8,128)(2,1)S(1)}, bf16[9,256,74]{1,2,0:T(8,128)(2,1)}, u32[]{:S(2)}) copy-start(bf16[9,256,74]{1,2,0:T(8,128)(2,1)} %param.12) | copy-start | bytes 1022980
  36.0 2.0 copy-start
  38.1 39.8 %collective-permute-start.1 = (bf16[256,1,512]{2,0,1:T(8,128)(2,1)S(1)}, bf16[256,1,512]{2,0,1:T(8,128)(2,1)S(1)}, u32[]{:S(2)}, u32[]{:S(2)}) collective-permute-start(bf16[256,1,512]{2,0,1:T(8,128)(2,1)S(1)} %get-tuple-element.41), channel_id=1, source_target_pairs={{1,0},{2,1},{3,2},{4,3},{5,4},{6,5},{7,6},{8,7},{9,8},{10,9},{11,1... | collective-permute-start | bytes 786440 | tf_op jit(solution)/shard_map/ppermute | solution.py:425
  41.1 49.1 %collective-permute-start = (bf16[256,1,512]{2,0,1:T(8,128)(2,1)S(1)}, bf16[256,1,512]{2,0,1:T(8,128)(2,1)S(1)}, u32[]{:S(2)}, u32[]{:S(2)}) collective-permute-start(bf16[256,1,512]{2,0,1:T(8,128)(2,1)S(1)} %get-tuple-element.40), channel_id=1, source_target_pairs={{0,1},{1,2},{2,3},{3,4},{4,5},{5,6},{6,7},{7,8},{8,9},{9,10},{10,1... | collective-permute-start | bytes 786440 | tf_op jit(solution)/shard_map/ppermute | solution.py:424
  43.7 48.6 %copy-start.1 = (bf16[3,3,256,80]{2,3,1,0:T(8,128)(2,1)}, bf16[3,3,256,80]{2,3,1,0:T(8,128)(2,1)S(1)}, u32[]{:S(2)}) copy-start(bf16[3,3,256,80]{2,3,1,0:T(8,128)(2,1)S(1)} %pad.4) | copy-start | bytes 1105924
  92.8 4.3 %collective-permute-start.3 = (bf16[256,18,1]{0,1,2:T(8,128)(2,1)S(1)}, bf16[256,18,1]{0,1,2:T(8,128)(2,1)S(1)}, u32[]{:S(2)}, u32[]{:S(2)}) collective-permute-start(bf16[256,18,1]{0,1,2:T(8,128)(2,1)S(1)} %copy.57), channel_id=1, source_target_pairs={{0,32},{32,64},{64,96},{96,0},{1,33},{33,65},{65,97},{97,1},{2,34}... | collective-permute-start | bytes 27656 | tf_op jit(solution)/shard_map/ppermute | solution.py:428
  95.3 2.8 collective-permute-start.2
  173.9 12.7 %copy-start.3 = (s32[64,4]{0,1:T(4,128)S(1)}, s32[64,4]{0,1:T(4,128)}, u32[]{:S(2)}) copy-start(s32[64,4]{0,1:T(4,128)} %param.9) | copy-start | bytes 3076
  173.9 12.9 %copy-start.4 = (s32[64]{0:T(128)S(1)}, s32[64]{0:T(128)}, u32[]{:S(2)}) copy-start(s32[64]{0:T(128)} %param.11) | copy-start | bytes 772
  173.9 76.5 %all-to-all-start.1 = ((bf16[128,160,128]{2,1,0:T(8,128)(2,1)}), bf16[128,160,128]{2,1,0:T(8,128)(2,1)}, u32[]{:S(2)}, u32[]{:S(2)}) async-start(bf16[128,160,128]{2,1,0:T(8,128)(2,1)} %reply.1), calls=%async_computation.1 | async-start | bytes 10485760 | tf_op jit(solution)/shard_map/all_to_all | solution.py:418
  252.6 37.2 %all-to-all-start.2 = ((bf16[128,11,128]{2,1,0:T(8,128)(2,1)}), bf16[128,11,128]{2,1,0:T(8,128)(2,1)S(1)}, u32[]{:S(2)}, u32[]{:S(2)}) async-start(bf16[128,11,128]{2,1,0:T(8,128)(2,1)} %broadcast_in_dim.41), calls=%async_computation.2 | async-start | bytes 1048576 | tf_op jit(solution)/shard_map/all_to_all | solution.py:418

commit v3 on v2

--- a/solution.py
+++ b/solution.py
@@ -1,4 +1,3 @@
-import functools
 import math
 
 import jax
@@ -7,6 +6,7 @@
 from jax.experimental import pallas as pl
 from jax.experimental.pallas import tpu as pltpu
 from jax.sharding import PartitionSpec as P
+
 
 C = 74
 CP = 80
@@ -19,7 +19,8 @@
 K = 4
 PIECES = 64
 DEVS = 128
-GRP = 8
+GRP = 32
+SUB = 8
 SHARE = 11
 BACK = 160
 VMEM_LIMIT = 63 * 1024 * 1024
@@ -37,18 +38,30 @@
     return pl.BlockSpec(shape, lambda *a: zeros)
 
 
-def partial_kernel(key_ref, lat_ref, w_ref, out_ref):
+def partial_kernel(key_ref, lat_ref, w_ref, out_ref, rows_ref):
     step = pl.program_id(0)
-    for g in range(GRP):
-        parts = []
-        for s in range(2):
-            key = key_ref[(step * GRP + g) * 2 + s]
-            entry = key >> 7
-            alive = (key & 1).astype(f32)
-            piece = ((key >> 1) & 63).astype(f32)
-            value = jnp.dot(lat_ref[entry >> 2], w_ref[entry], preferred_element_type=f32)
-            parts += [value * alive, jnp.full((SL - C, PP), piece, f32)]
-        out_ref[g] = jnp.concatenate(parts, axis=0).astype(bf16)
+    blocks = lat_ref.shape[1]
+
+    @pl.when(step == 0)
+    def _():
+        for c in range(C):
+            rows_ref[c * blocks : (c + 1) * blocks] = lat_ref[c].astype(f32)
+
+    def body(i, carry):
+        for g in range(SUB):
+            parts = []
+            for s in range(2):
+                key = key_ref[(step * GRP + i * SUB + g) * 2 + s]
+                entry = key >> 7
+                alive = (key & 1).astype(f32)
+                piece = ((key >> 1) & 63).astype(f32)
+                lat = rows_ref[pl.ds(entry >> 2, C, stride=blocks), :].astype(bf16)
+                value = jnp.dot(lat, w_ref[entry], preferred_element_type=f32)
+                parts += [value * alive, jnp.full((SL - C, PP), piece, f32)]
+            out_ref[i * SUB + g] = jnp.concatenate(parts, axis=0).astype(bf16)
+        return carry
+
+    lax.fori_loop(0, GRP // SUB, body, 0)
 
 
 def partial_products(keys, lat, weight):
@@ -59,6 +72,7 @@
             grid=(DEVS // GRP,),
             in_specs=[whole(lat.shape), whole(weight.shape)],
             out_specs=pl.BlockSpec((GRP, 2 * SL, PP), lambda i, *a: (i, 0, 0)),
+            scratch_shapes=[pltpu.VMEM((C * lat.shape[1], PP), f32)],
         ),
         out_shape=jax.ShapeDtypeStruct((DEVS, 2 * SL, PP), bf16),
         compiler_params=params(),
@@ -76,11 +90,15 @@
     def _():
         acc_ref[...] = jnp.zeros_like(acc_ref)
 
-    for g in range(GRP):
-        block = recv_ref[g].astype(f32)
-        for s in range(2):
-            piece = piece_ref[(step * GRP + g) * 2 + s]
-            acc_ref[piece, :SL] += block[s * SL : (s + 1) * SL]
+    def body(i, carry):
+        for g in range(SUB):
+            block = recv_ref[i * SUB + g].astype(f32)
+            for s in range(2):
+                piece = piece_ref[(step * GRP + i * SUB + g) * 2 + s]
+                acc_ref[piece, :SL] += block[s * SL : (s + 1) * SL]
+        return carry
+
+    lax.fori_loop(0, GRP // SUB, body, 0)
 
     @pl.when(step == pl.num_programs(0) - 1)
     def _():
@@ -340,15 +358,20 @@
 
 def reply_kernel(piece_ref, dfield_ref, rows_ref, out_ref):
     step = pl.program_id(0)
-    terms = rows_ref[...]
-    for g in range(GRP):
-        parts = []
-        for s in range(2):
-            piece = piece_ref[(step * GRP + g) * 2 + s]
-            parts.append(dfield_ref[piece].astype(f32)[:C])
-        parts.append(terms[g * SHARE : (g + 1) * SHARE])
-        parts.append(jnp.zeros((BACK - 2 * C - SHARE, PP), f32))
-        out_ref[g] = jnp.concatenate(parts, axis=0).astype(bf16)
+
+    def body(i, carry):
+        terms = rows_ref[pl.ds(pl.multiple_of(i * (SUB * SHARE), 8), SUB * SHARE)]
+        for g in range(SUB):
+            parts = []
+            for s in range(2):
+                piece = piece_ref[(step * GRP + i * SUB + g) * 2 + s]
+                parts.append(dfield_ref[piece].astype(f32)[:C])
+            parts.append(terms[g * SHARE : (g + 1) * SHARE])
+            parts.append(jnp.zeros((BACK - 2 * C - SHARE, PP), f32))
+            out_ref[i * SUB + g] = jnp.concatenate(parts, axis=0).astype(bf16)
+        return carry
+
+    lax.fori_loop(0, GRP // SUB, body, 0)
 
 
 def replies(pieces, dfield, rows):
@@ -369,26 +392,45 @@
     )(pieces, dfield, rows)
 
 
-def final_kernel(place_ref, back_hbm, w_ref, out_ref, back_ref, sem):
+def final_kernel(place_ref, back_hbm, w_ref, out_ref, back_ref, rows_ref, sem):
     step = pl.program_id(0)
+    blocks = out_ref.shape[1]
+    part = DEVS // 4
 
     @pl.when(step == 0)
     def _():
-        copy = pltpu.make_async_copy(back_hbm, back_ref, sem)
-        copy.start()
-        copy.wait()
-
-    for g in range(4):
-        total = jnp.zeros((C, PP), f32)
-        for j in range(K):
-            code = place_ref[(step * 4 + g) * K + j]
-            both = back_ref[code >> 2].astype(f32)
-            got = jnp.where(((code >> 1) & 1) == 0, both[:C], both[C : 2 * C])
-            got = (got * (code & 1).astype(f32)).astype(bf16)
-            total += lax.dot_general(
-                got, w_ref[g, j], (((1,), (1,)), ((), ())), preferred_element_type=f32
+        copies = [
+            pltpu.make_async_copy(
+                back_hbm.at[pl.ds(i * part, part)], back_ref.at[pl.ds(i * part, part)], sem.at[i]
             )
-        out_ref[g] = total.astype(bf16)
+            for i in range(4)
+        ]
+        for copy in copies:
+            copy.start()
+        for copy in copies:
+            copy.wait()
+
+    def body(i, carry):
+        for g in range(4):
+            here = i * 4 + g
+            total = jnp.zeros((C, PP), f32)
+            for j in range(K):
+                code = place_ref[(step * 16 + here) * K + j]
+                both = back_ref[code >> 2].astype(f32)
+                got = jnp.where(((code >> 1) & 1) == 0, both[:C], both[C : 2 * C])
+                got = (got * (code & 1).astype(f32)).astype(bf16)
+                total += lax.dot_general(
+                    got, w_ref[here, j], (((1,), (1,)), ((), ())), preferred_element_type=f32
+                )
+            rows_ref[pl.ds(step * 16 + here, C, stride=blocks), :] = total
+        return carry
+
+    lax.fori_loop(0, 4, body, 0)
+
+    @pl.when(step == pl.num_programs(0) - 1)
+    def _():
+        for c in range(C):
+            out_ref[c] = rows_ref[c * blocks : (c + 1) * blocks].astype(bf16)
 
 
 def final_products(places, back, weight):
@@ -397,15 +439,19 @@
         final_kernel,
         grid_spec=pltpu.PrefetchScalarGridSpec(
             num_scalar_prefetch=1,
-            grid=(blocks // 4,),
+            grid=(blocks // 16,),
             in_specs=[
                 pl.BlockSpec(memory_space=pltpu.HBM),
-                pl.BlockSpec((4, K, PP, PP), lambda i, *a: (i, 0, 0, 0)),
+                pl.BlockSpec((16, K, PP, PP), lambda i, *a: (i, 0, 0, 0)),
             ],
-            out_specs=pl.BlockSpec((4, C, PP), lambda i, *a: (i, 0, 0)),
-            scratch_shapes=[pltpu.VMEM(back.shape, bf16), pltpu.SemaphoreType.DMA],
-        ),
-        out_shape=jax.ShapeDtypeStruct((blocks, C, PP), bf16),
+            out_specs=whole((C, blocks, PP)),
+            scratch_shapes=[
+                pltpu.VMEM(back.shape, bf16),
+                pltpu.VMEM((C * blocks, PP), f32),
+                pltpu.SemaphoreType.DMA((4,)),
+            ],
+        ),
+        out_shape=jax.ShapeDtypeStruct((C, blocks, PP), bf16),
         compiler_params=params(),
         cost_estimate=pl.CostEstimate(
             flops=1_300_000_000, bytes_accessed=30_000_000, transcendentals=0
@@ -453,7 +499,7 @@
 
     cots = cotangent_rim(cotangent[0])
     send = partial_products(
-        keys, latlon, intersection_weight.reshape(blocks * K, PP, PP)
+        keys, latlon.transpose(1, 0, 2), intersection_weight.reshape(blocks * K, PP, PP)
     )
     recv = exchange(send)
     pieces = jnp.stack([recv[:, C, 0], recv[:, SL + C, 0]], axis=1).reshape(-1).astype(jnp.int32)
@@ -466,15 +512,15 @@
     wb = kernel.transpose(0, 1, 3, 2).reshape(3, 3 * CP, HID)
     meta = lax.axis_index("tile").astype(jnp.int32).reshape(1)
     act, rows, dfield = conv(meta, field, top, bottom, side, wf, wb, cots)
+    reply = replies(pieces, dfield, rows)
     activation = channel_major(act)[None]
-
-    back = exchange(replies(pieces, dfield, rows))
+    back = exchange(reply)
     share = jnp.sum(back[:, 2 * C : 2 * C + SHARE].astype(f32), axis=0)
     share = (share * (1.0 / math.sqrt(DEVS * ROWS * COLS))).astype(bf16)
     summed = exchange(jnp.broadcast_to(share[None], (DEVS, SHARE, PP)))
     summed = summed.reshape(DEVS * SHARE, PP)[: 18 * C].reshape(2, 9, C, PP)
     grad_conv = summed.astype(f32).transpose(1, 0, 3, 2).reshape(9, HID, C)
-    grad_latlon = final_products(places, back, intersection_weight)
+    grad_latlon = final_products(places, back, intersection_weight).transpose(1, 0, 2)
     return (activation, grad_conv, grad_latlon)
 
 

time: 294 us -> 280 us (0.952)
  Pallas kernels: 110 us -> 102 us
  local copies, waits for them, and re-layouts: 22.6 us -> 16.8 us
    unnamed x14 -> x12, local copies, waits for them, and re-layouts: 12.5 us -> 6.7 us
    pallas_call x1, Pallas kernels: 10.8 us -> 5.75 us  [replies(): pl.pallas_call(reply_kernel, grid_spec=pltpu.PrefetchScalarGridSpec(num_s...]
    pallas_call x1, Pallas kernels: 13.4 us -> 18.3 us  [partial_products(): pl.pallas_call(partial_kernel, grid_spec=pltpu.PrefetchScalarGridSpec(num...]
    pallas_call x1, Pallas kernels: 11 us -> 6.2 us  [gather_field(): pl.pallas_call(gather_kernel, grid_spec=pltpu.PrefetchScalarGridSpec(num_...]
  transfers between devices with their start and end apart: 7 -> 7, of which waited for: 4 -> 4; matrix products, arithmetic and copies ran while one was open for 6% -> 5% of each run, Pallas kernels for 9% -> 8%
where the time goes in v3:
time: 280 us; the launch traced here: 279 us
  waiting for transfers between devices  109 us (39%)
  Pallas kernels  102 us (36%)
  starting transfers between devices  41.1 us (15%)
  local copies, waits for them, and re-layouts  16.8 us (6%)
  other arithmetic  8.24 us (3%)
    all_to_all x3, waiting for transfers between devices, exchange(): lax.all_to_all(value, ('face', 'tile'), split_axis=0, concat_axis=0, tile...  63.6 us
    pallas_call x1, Pallas kernels, conv(): pl.pallas_call(conv_kernel, grid_spec=pltpu.PrefetchScalarGridSpec(num_sc...  37.1 us
    ppermute x1, waiting for transfers between devices, cotangent_rim(): below = lax.ppermute(cot[:, :1], 'tile', down)  33.1 us
    all_to_all x3, starting transfers between devices, exchange(): lax.all_to_all(value, ('face', 'tile'), split_axis=0, concat_axis=0, tile...  32.6 us
    pallas_call x1, Pallas kernels, partial_products(): pl.pallas_call(partial_kernel, grid_spec=pltpu.PrefetchScalarGridSpec(num...  18.3 us
    pallas_call x1, Pallas kernels, final_products(): pl.pallas_call(final_kernel, grid_spec=pltpu.PrefetchScalarGridSpec(num_s...  14.7 us
    ppermute x1, waiting for transfers between devices, cotangent_rim(): above = lax.ppermute(cot[:, ROWS - 1:], 'tile', up)  12.4 us
    pallas_call x1, Pallas kernels, halo(): pl.pallas_call(halo_kernel, in_specs=[vmem, vmem], out_specs=[vmem, vmem,...  11.8 us
  transfers between devices with their start and end apart: 7, of which 4 were waited for; matrix products, arithmetic and copies ran while one was open for 5% of the time, Pallas kernels for 8%

profile of v3, /device:TPU:1, one launch (start us, length us, event | category | flops | bytes accessed | tf_op | source)
XLA Modules:
  0.0 278.6 jit_solution(14337016835745522811)
XLA Ops:
  3.0 18.3 %partial.1 = bf16[128,152,128]{2,1,0:T(8,128)(2,1)} custom-call(s32[256]{0:T(256)} %reshape.68.key_ref, bf16[74,64,128]{2,1,0:T(8,128)(2,1)} %bitcast.37, bf16[256,128,128]{2,1,0:T(8,128)(2,1)} %bitcast.32), custom_call_target="tpu_custom_call" | custom-call | flops 1300000000 | bytes 15000000 | tf_op jit(solution)/shard_map/partial/pallas_call | solution.py:68
  21.2 11.9 %all-to-all-start = ((bf16[128,152,128]{2,1,0:T(8,128)(2,1)}), bf16[128,152,128]{2,1,0:T(8,128)(2,1)}, u32[]{:S(2)}, u32[]{:S(2)}) async-start(bf16[128,152,128]{2,1,0:T(8,128)(2,1)} %partial.1), calls=%async_computation | async-start | bytes 9961472 | tf_op jit(solution)/shard_map/all_to_all | solution.py:464
  33.1 4.6 %copy.57 = bf16[1,256,16,512]{3,1,2,0:T(8,128)(2,1)S(1)} copy(bf16[1,256,16,512]{3,2,1,0:T(8,128)(2,1)} %param.13) | data formatting | bytes 8388608 | tf_op args[6]
  37.7 2.0 copy-done
  39.8 3.0 %collective-permute-start.1 = (bf16[256,1,512]{2,0,1:T(8,128)(2,1)S(1)}, bf16[256,1,512]{2,0,1:T(8,128)(2,1)S(1)}, u32[]{:S(2)}, u32[]{:S(2)}) collective-permute-start(bf16[256,1,512]{2,0,1:T(8,128)(2,1)S(1)} %get-tuple-element.26), channel_id=1, source_target_pairs={{1,0},{2,1},{3,2},{4,3},{5,4},{6,5},{7,6},{8,7},{9,8},{10,9},{11,1... | collective-permute-start | bytes 786440 | tf_op jit(solution)/shard_map/ppermute | solution.py:471
  42.8 2.5 collective-permute-start
  46.4 33.1 %collective-permute-done.1 = bf16[256,1,512]{2,0,1:T(8,128)(2,1)S(1)} collective-permute-done((bf16[256,1,512]{2,0,1:T(8,128)(2,1)S(1)}, bf16[256,1,512]{2,0,1:T(8,128)(2,1)S(1)}, u32[]{:S(2)}, u32[]{:S(2)}) %collective-permute-start.1) | collective-permute-done | bytes 262176 | tf_op jit(solution)/shard_map/ppermute | solution.py:471
  79.5 12.4 %collective-permute-done = bf16[256,1,512]{2,0,1:T(8,128)(2,1)S(1)} collective-permute-done((bf16[256,1,512]{2,0,1:T(8,128)(2,1)S(1)}, bf16[256,1,512]{2,0,1:T(8,128)(2,1)S(1)}, u32[]{:S(2)}, u32[]{:S(2)}) %collective-permute-start) | collective-permute-done | bytes 262176 | tf_op jit(solution)/shard_map/ppermute | solution.py:470
  91.9 2.0 pad_maximum_fusion.2
  94.5 1.9 collective-permute-start.3
  96.9 1.1 collective-permute-start.2
  100.3 1.7 maximum_bitcast_fusion.edge_ref
  102.0 2.1 slice_reduce_fusion.1
  104.9 6.2 %gather_field.1 = (bf16[64,80,128]{2,1,0:T(8,128)(2,1)}, bf16[2,80,128]{2,1,0:T(8,128)(2,1)}) custom-call(s32[256]{0:T(256)} %reshape.77.piece_ref, bf16[128,152,128]{2,1,0:T(8,128)(2,1)} %all-to-all-done.recv_ref), custom_call_target="tpu_custom_call" | custom-call | tf_op jit(solution)/shard_map/gather_field/pallas_call | solution.py:123
  111.1 11.8 %halo.1 = (bf16[8,80,128]{2,1,0:T(8,128)(2,1)}, bf16[8,80,128]{2,1,0:T(8,128)(2,1)}, bf16[6,80,128]{2,1,0:T(8,128)(2,1)}) custom-call(bf16[64,80,128]{2,1,0:T(8,128)(2,1)} %get-tuple-element.11.field_ref, bf16[2,80,128]{2,1,0:T(8,128)(2,1)} %get-tuple-element.12.pack_ref), custom_call_target="tpu_custom_call" | custom-call | tf_op jit(solution)/shard_map/halo/pallas_call | solution.py:178
  122.9 37.1 %conv.1 = (bf16[16,256,512]{2,1,0:T(8,128)(2,1)}, f32[1408,128]{1,0:T(8,128)}, bf16[64,80,128]{2,1,0:T(8,128)(2,1)}) custom-call(s32[1]{0:T(128)} %bitcast.meta_ref, bf16[64,80,128]{2,1,0:T(8,128)(2,1)} %get-tuple-element.11.field_ref, bf16[8,80,128]{2,1,0:T(8,128)(2,1)} %get-tuple-element.13.top_ref, bf16[8,80,128]{2,1,0:T(8,128)(2,1)} %get-tuple-element.14.bottom_ref, ...), custom_call_target="tpu_custom_call" | custom-call | tf_op jit(solution)/shard_map/conv/pallas_call | solution.py:288
  160.0 5.7 %reply.1 = bf16[128,160,128]{2,1,0:T(8,128)(2,1)} custom-call(s32[256]{0:T(256)} %reshape.77.piece_ref, bf16[64,80,128]{2,1,0:T(8,128)(2,1)} %get-tuple-element.17.dfield_ref, f32[1408,128]{1,0:T(8,128)} %get-tuple-element.18.rows_ref), custom_call_target="tpu_custom_call" | custom-call | tf_op jit(solution)/shard_map/reply/pallas_call | solution.py:378
  165.8 12.7 %all-to-all-start.1 = ((bf16[128,160,128]{2,1,0:T(8,128)(2,1)}), bf16[128,160,128]{2,1,0:T(8,128)(2,1)}, u32[]{:S(2)}, u32[]{:S(2)}) async-start(bf16[128,160,128]{2,1,0:T(8,128)(2,1)} %reply.1), calls=%async_computation.1 | async-start | bytes 10485760 | tf_op jit(solution)/shard_map/all_to_all | solution.py:464
  178.7 63.6 %all-to-all-done.1.back_hbm = bf16[128,160,128]{2,1,0:T(8,128)(2,1)} async-done(((bf16[128,160,128]{2,1,0:T(8,128)(2,1)}), bf16[128,160,128]{2,1,0:T(8,128)(2,1)}, u32[]{:S(2)}, u32[]{:S(2)}) %all-to-all-start.1) | async-done | bytes 5242912 | tf_op jit(solution)/shard_map/all_to_all | solution.py:464
  242.3 1.3 convert_reduce_fusion
  244.4 8.0 %all-to-all-start.2 = ((bf16[128,11,128]{2,1,0:T(8,128)(2,1)}), bf16[128,11,128]{2,1,0:T(8,128)(2,1)S(1)}, u32[]{:S(2)}, u32[]{:S(2)}) async-start(bf16[128,11,128]{2,1,0:T(8,128)(2,1)} %broadcast_in_dim.41), calls=%async_computation.2 | async-start | bytes 1048576 | tf_op jit(solution)/shard_map/all_to_all | solution.py:464
  253.4 8.4 %channel_major.1 = bf16[256,16,512]{2,1,0:T(8,128)(2,1)} custom-call(bf16[16,256,512]{2,1,0:T(8,128)(2,1)} %get-tuple-element.16.in_ref), custom_call_target="tpu_custom_call" | custom-call | flops 20000000 | bytes 160000000 | tf_op jit(solution)/shard_map/channel_major/pallas_call | solution.py:344
  261.9 14.7 %final.1 = bf16[74,64,128]{2,1,0:T(8,128)(2,1)} custom-call(s32[256]{0:T(256)} %add_add_fusion.place_ref, bf16[128,160,128]{2,1,0:T(8,128)(2,1)} %all-to-all-done.1.back_hbm, bf16[64,4,128,128]{3,2,1,0:T(8,128)(2,1)} %w_ref.1), custom_call_target="tpu_custom_call" | custom-call | flops 1300000000 | bytes 30000000 | tf_op jit(solution)/shard_map/final/pallas_call | solution.py:438
  277.2 1.4 reshape.79
  (44 shorter events, 10.2 us)
Async XLA Ops:
  21.2 80.8 %all-to-all-start = ((bf16[128,152,128]{2,1,0:T(8,128)(2,1)}), bf16[128,152,128]{2,1,0:T(8,128)(2,1)}, u32[]{:S(2)}, u32[]{:S(2)}) async-start(bf16[128,152,128]{2,1,0:T(8,128)(2,1)} %partial.1), calls=%async_computation | async-start | bytes 9961472 | tf_op jit(solution)/shard_map/all_to_all | solution.py:464
  33.1 12.3 %copy-start.2 = (bf16[9,256,74]{1,2,0:T(8,128)(2,1)S(1)}, bf16[9,256,74]{1,2,0:T(8,128)(2,1)}, u32[]{:S(2)}) copy-start(bf16[9,256,74]{1,2,0:T(8,128)(2,1)} %param.12) | copy-start | bytes 1022980
  37.7 2.0 copy-start
  39.8 39.8 %collective-permute-start.1 = (bf16[256,1,512]{2,0,1:T(8,128)(2,1)S(1)}, bf16[256,1,512]{2,0,1:T(8,128)(2,1)S(1)}, u32[]{:S(2)}, u32[]{:S(2)}) collective-permute-start(bf16[256,1,512]{2,0,1:T(8,128)(2,1)S(1)} %get-tuple-element.26), channel_id=1, source_target_pairs={{1,0},{2,1},{3,2},{4,3},{5,4},{6,5},{7,6},{8,7},{9,8},{10,9},{11,1... | collective-permute-start | bytes 786440 | tf_op jit(solution)/shard_map/ppermute | solution.py:471
  42.8 49.1 %collective-permute-start = (bf16[256,1,512]{2,0,1:T(8,128)(2,1)S(1)}, bf16[256,1,512]{2,0,1:T(8,128)(2,1)S(1)}, u32[]{:S(2)}, u32[]{:S(2)}) collective-permute-start(bf16[256,1,512]{2,0,1:T(8,128)(2,1)S(1)} %get-tuple-element.25), channel_id=1, source_target_pairs={{0,1},{1,2},{2,3},{3,4},{4,5},{5,6},{6,7},{7,8},{8,9},{9,10},{10,1... | collective-permute-start | bytes 786440 | tf_op jit(solution)/shard_map/ppermute | solution.py:470
  45.4 48.6 %copy-start.1 = (bf16[3,3,256,80]{2,3,1,0:T(8,128)(2,1)}, bf16[3,3,256,80]{2,3,1,0:T(8,128)(2,1)S(1)}, u32[]{:S(2)}) copy-start(bf16[3,3,256,80]{2,3,1,0:T(8,128)(2,1)S(1)} %pad.4) | copy-start | bytes 1105924
  94.5 4.3 %collective-permute-start.3 = (bf16[256,18,1]{0,1,2:T(8,128)(2,1)S(1)}, bf16[256,18,1]{0,1,2:T(8,128)(2,1)S(1)}, u32[]{:S(2)}, u32[]{:S(2)}) collective-permute-start(bf16[256,18,1]{0,1,2:T(8,128)(2,1)S(1)} %copy.48), channel_id=1, source_target_pairs={{0,32},{32,64},{64,96},{96,0},{1,33},{33,65},{65,97},{97,1},{2,34}... | collective-permute-start | bytes 27656 | tf_op jit(solution)/shard_map/ppermute | solution.py:474
  96.9 2.8 collective-permute-start.2
  165.8 12.7 %copy-start.3 = (s32[64,4]{0,1:T(4,128)S(1)}, s32[64,4]{0,1:T(4,128)}, u32[]{:S(2)}) copy-start(s32[64,4]{0,1:T(4,128)} %param.9) | copy-start | bytes 3076
  165.8 12.9 %copy-start.4 = (s32[64]{0:T(128)S(1)}, s32[64]{0:T(128)}, u32[]{:S(2)}) copy-start(s32[64]{0:T(128)} %param.11) | copy-start | bytes 772
  165.8 76.5 %all-to-all-start.1 = ((bf16[128,160,128]{2,1,0:T(8,128)(2,1)}), bf16[128,160,128]{2,1,0:T(8,128)(2,1)}, u32[]{:S(2)}, u32[]{:S(2)}) async-start(bf16[128,160,128]{2,1,0:T(8,128)(2,1)} %reply.1), calls=%async_computation.1 | async-start | bytes 10485760 | tf_op jit(solution)/shard_map/all_to_all | solution.py:464
  244.4 32.1 %all-to-all-start.2 = ((bf16[128,11,128]{2,1,0:T(8,128)(2,1)}), bf16[128,11,128]{2,1,0:T(8,128)(2,1)S(1)}, u32[]{:S(2)}, u32[]{:S(2)}) async-start(bf16[128,11,128]{2,1,0:T(8,128)(2,1)} %broadcast_in_dim.41), calls=%async_computation.2 | async-start | bytes 1048576 | tf_op jit(solution)/shard_map/all_to_all | solution.py:464
